TPU v7x, 32 devices: a whole 2x2x4 slice. The times are simulated.
32 devices in a mesh: groups: 2 (over y), state: 4 (over z), type: 4 (over x, core).
Axes of the slice: x: 2, y: 2, z: 4, core: 2. Of those that a mesh axis runs over, the one named last changes fastest.
Arguments:
- value_in: bfloat16 [16384, 2048], P(('groups', 'state'), 'type'), parts along dimension 0, may hold values from -7.5 to 7.5
- cotangent: bfloat16 [16384, 2048], P(('groups', 'state'), 'type'), parts along dimension 0, may hold values from -100 to 100
- state_util: float32 [2, 16384], P(None, ('groups', 'state')), parts along dimension 1, may hold values from -300 to 300
- taste: float32 [2, 4096], P(None, ('groups', 'type')), parts along dimension 1, may hold values from -6 to 6
- tiles: bfloat16 [128, 2, 6, 128, 128], P(('groups', 'state')), parts along dimension 0, may hold values from 0 to 0.0051879883
- dest_block: int32 [128, 2, 6], P(('groups', 'state')), parts along dimension 0, may hold values from 0 to 63, as said below
- counts: int32 [128, 2], P(('groups', 'state')), parts along dimension 0, may hold values from 1 to 6
Outputs:
- value_out: float32 [16384, 2048], P(('groups', 'state'), 'type'), parts along dimension 0
- adjoint: float32 [16384, 2048], P(('groups', 'state'), 'type'), parts along dimension 0
- grad_util: float32 [2, 16384], P(None, ('groups', 'state')), parts along dimension 1
- grad_taste: float32 [2, 4096], P(None, ('groups', 'type')), parts along dimension 1
There are 2 independent parts, one for each index of `groups`. A program takes and returns all parts, laid end to end along the dimension named above; each array names one. Nothing has to cross between parts.
Inputs may be any that keep to these rules, and one draw needn't show every extreme that they name: `dest_block`: entries at or beyond a list's count name blocks of the list's own run of 16 blocks. In each run of 16 blocks exactly 16 used entries name blocks outside the run, at most 6 of them in any one other run, and exactly 6 in some other run.
All inputs are finite; a program needn't handle non-finite values.
Results may differ from a plain program's by a relative error of at most 0.0012.
Values may be sent and summed in bfloat16 or wider, within the bound.
A program may use at most 192 MiB of HBM per device.

v0:
```python
import jax
import jax.numpy as jnp
from jax import lax
from jax.sharding import PartitionSpec as P


def local(value_in, cotangent, state_util, taste, tiles, dest_block, counts):
    block_count, action_count, entry_count, tile_rows, _ = tiles.shape
    type_width = value_in.shape[1]
    device_count = lax.axis_size("state")
    my_index = lax.axis_index("state")
    capacity = max(2, (block_count + device_count - 2) // (device_count - 1))
    entry_total = block_count * action_count * entry_count
    value_blocks = value_in.reshape(block_count, tile_rows, type_width)
    flat_dest = dest_block.reshape(entry_total)
    owner = flat_dest // block_count
    local_block = flat_dest % block_count
    used = (jnp.arange(entry_count, dtype=jnp.int32)[None, None, :] < counts[:, :, None]).reshape(
        entry_total
    )
    remote = used & (owner != my_index)
    local_used = used & (owner == my_index)
    peer_ids = jnp.arange(device_count, dtype=jnp.int32)
    owner_hits = (remote[:, None] & (owner[:, None] == peer_ids[None, :])).astype(jnp.int32)
    earlier = jnp.cumsum(owner_hits, axis=0) - owner_hits
    slot_of = jnp.sum(earlier * owner_hits, axis=1)
    target = jnp.where(remote, owner * capacity + slot_of, device_count * capacity)
    request = (
        jnp.full((device_count * capacity,), -1, jnp.int32).at[target].set(local_block, mode="drop")
    )
    source_entry = (
        jnp.full((device_count * capacity,), -1, jnp.int32)
        .at[target]
        .set(jnp.arange(entry_total, dtype=jnp.int32), mode="drop")
    )
    wanted = lax.all_to_all(
        request.reshape(device_count, capacity), "state", split_axis=0, concat_axis=0, tiled=True
    )
    outgoing = jnp.take(value_blocks, jnp.clip(wanted.reshape(-1), 0, block_count - 1), axis=0)
    incoming = lax.all_to_all(
        outgoing.reshape(device_count, capacity, tile_rows, type_width),
        "state",
        split_axis=0,
        concat_axis=0,
        tiled=True,
    )
    table = jnp.concatenate(
        [value_blocks, incoming.reshape(device_count * capacity, tile_rows, type_width)], axis=0
    )
    lookup = jnp.where(remote, block_count + target, local_block)
    picked = jnp.take(table, lookup, axis=0)
    picked = jnp.where(used[:, None, None], picked, jnp.zeros_like(picked))
    picked = picked.reshape(block_count, action_count, entry_count, tile_rows, type_width)
    cont = jnp.einsum("bamij,bamjk->baik", tiles, picked, preferred_element_type=jnp.float32)
    util_grid = state_util.reshape(action_count, block_count, tile_rows).transpose(1, 0, 2)[
        :, :, :, None
    ]
    scores = util_grid + taste[None, :, None, :] + 0.95 * cont
    largest = jnp.max(scores, axis=1)
    value = largest + jnp.log(jnp.sum(jnp.exp(scores - largest[:, None]), axis=1))
    prob = jnp.exp(scores - value[:, None])
    grad_q = cotangent.reshape(block_count, 1, tile_rows, type_width).astype(jnp.float32) * prob
    util_part = (
        jnp.sum(grad_q, axis=3).transpose(1, 0, 2).reshape(action_count, block_count * tile_rows)
    )
    util_total = lax.psum(util_part, "type") / (type_width * lax.axis_size("type"))
    taste_total = lax.psum(jnp.sum(grad_q, axis=(0, 2)), "state") / (
        block_count * tile_rows * device_count
    )
    scaled = (0.95 * grad_q).astype(jnp.bfloat16)
    slot_valid = source_entry >= 0
    safe_entry = jnp.clip(source_entry, 0, entry_total - 1)
    contrib = jnp.einsum(
        "bamij,baik->bamjk", tiles, scaled, preferred_element_type=jnp.float32
    ).reshape(entry_total, tile_rows, type_width)
    outbound = jnp.where(
        slot_valid[:, None, None], jnp.take(contrib, safe_entry, axis=0), 0.0
    ).astype(jnp.bfloat16)
    returned = lax.all_to_all(
        outbound.reshape(device_count, capacity, tile_rows, type_width),
        "state",
        split_axis=0,
        concat_axis=0,
        tiled=True,
    )
    block_ids = jnp.arange(block_count, dtype=jnp.int32)
    local_select = (local_used[:, None] & (local_block[:, None] == block_ids[None, :])).astype(
        jnp.float32
    )
    own_terms = jnp.einsum("rd,rjk->djk", local_select, contrib, precision=lax.Precision.HIGHEST)
    arrive_select = (wanted.reshape(-1)[None, :] == block_ids[:, None]).astype(jnp.bfloat16)
    arrived = jnp.dot(
        arrive_select,
        returned.reshape(device_count * capacity, tile_rows * type_width),
        preferred_element_type=jnp.float32,
    )
    adjoint = own_terms + arrived.reshape(block_count, tile_rows, type_width)
    value_out = value.reshape(block_count * tile_rows, type_width)
    return (
        value_out,
        adjoint.reshape(block_count * tile_rows, type_width),
        util_total,
        taste_total,
    )


def solution(mesh):
    return jax.shard_map(
        local,
        mesh=mesh,
        in_specs=(
            P(("groups", "state"), "type"),
            P(("groups", "state"), "type"),
            P(None, ("groups", "state")),
            P(None, ("groups", "type")),
            P(("groups", "state"), None, None, None, None),
            P(("groups", "state"), None, None),
            P(("groups", "state"), None),
        ),
        out_specs=(
            P(("groups", "state"), "type"),
            P(("groups", "state"), "type"),
            P(None, ("groups", "state")),
            P(None, ("groups", "type")),
        ),
        check_vma=False,
    )
```

profile of v0, /device:TPU:0, one launch (start us, length us, event | category | flops | bytes accessed | tf_op | source)
XLA Modules:
  0.0 337.9 jit_solution(11441029719686296648)
XLA Ops:
  0.6 0.8 copy.37
  1.4 0.1 iota_compare_fusion.1
  1.5 0.1 lt.106
  1.6 0.1 lt.109
  1.7 0.8 copy.38
  2.5 0.1 reshape.392
  2.6 0.1 reshape.396
  2.8 1.2 reduce-window.6
  4.1 0.1 copy.43
  4.3 0.1 copy.44
  4.5 1.2 scatter_custom_fusion
  5.7 0.1 all_to_all.12
  5.8 11.7 %all_to_all.19 = s32[4,1,6]{2,1,0:T(1,128)S(1)} all-to-all(s32[4,1,6]{2,1,0:T(1,128)S(1)} %bitcast.86), channel_id=1, replica_groups=mesh['groups'=2,'state'=4,'type'=4] {'state'}, dimensions={0} | all-to-all | bytes 192 | tf_op jit(solution)/shard_map/all_to_all | solution.py:36
  17.5 0.5 broadcast.505
  18.0 0.7 fusion.47
  18.7 0.1 min.24
  18.8 2.3 gather_fusion
  21.1 2.0 broadcast_select_fusion
  23.2 4.8 %all-to-all-start.1 = ((bf16[4,6,128,512]{3,2,1,0:T(8,128)(2,1)}), bf16[4,6,128,512]{3,2,1,0:T(8,128)(2,1)}, u32[]{:S(2)}, u32[]{:S(2)}) async-start(bf16[4,6,128,512]{3,2,1,0:T(8,128)(2,1)} %broadcast_select_fusion), calls=%async_computation.1 | async-start | bytes 6291456 | tf_op jit(solution)/shard_map/all_to_all | solution.py:40
  28.0 0.1 reduce_sum.41
  28.1 1.4 scatter_custom_fusion.1
  29.5 0.1 broadcast_in_dim.91
  29.6 0.1 broadcast_in_dim.89
  29.7 4.1 %copy.49 = f32[16,128,512]{1,2,0:T(8,128)} copy(bf16[16,128,512]{2,1,0:T(8,128)(2,1)} %bitcast.81) | data formatting | bytes 6291456 | tf_op jit(solution)/shard_map/convert_element_type | solution.py:62
  33.8 0.1 compare_and_fusion
  33.9 63.7 %all-to-all-done.1 = bf16[4,6,128,512]{3,2,1,0:T(8,128)(2,1)} async-done(((bf16[4,6,128,512]{3,2,1,0:T(8,128)(2,1)}), bf16[4,6,128,512]{3,2,1,0:T(8,128)(2,1)}, u32[]{:S(2)}, u32[]{:S(2)}) %all-to-all-start.1) | async-done | bytes 3145760 | tf_op jit(solution)/shard_map/all_to_all | solution.py:40
  97.5 4.7 %pad_maximum_fusion = bf16[40,128,512]{2,1,0:T(8,128)(2,1)} fusion(bf16[24,128,512]{2,1,0:T(8,128)(2,1)} %bitcast.11, bf16[16,128,512]{2,1,0:T(8,128)(2,1)S(1)} %bitcast.75), kind=kLoop, calls=%fused_computation.20 | loop fusion | flops 2621440 | bytes 10485760 | tf_op jit(solution)/shard_map/concatenate | solution.py:47
  102.3 13.6 %gather_fusion.1 = bf16[192,128,512]{2,1,0:T(8,128)(2,1)} fusion(bf16[40,128,512]{2,1,0:T(8,128)(2,1)} %pad_maximum_fusion, s32[1024]{0:T(1024)S(1)} %pad_clamp_fusion.1), kind=kCustom, calls=%fused_computation.1 | custom fusion | bytes 50332416 | tf_op jit(solution)/shard_map/jit(_take)/gather | solution.py:51
  115.8 32.6 %copy.47 = bf16[16,2,6,128,512]{3,4,2,1,0:T(8,128)(2,1)} copy(bf16[16,2,6,128,512]{4,3,2,1,0:T(8,128)(2,1)} %bitcast.73) | data formatting | bytes 50331648 | tf_op jit(solution)/shard_map/jit(_take)/gather | solution.py:51
  148.4 15.0 %fusion.48 = (f32[16,128,512]{1,2,0:T(8,128)}, f32[16,2,128,512]{2,3,1,0:T(8,128)S(1)}) fusion(bf16[16,2,6,128,128]{4,3,2,1,0:T(8,128)(2,1)} %param.11, bf16[16,2,6,128,512]{3,4,2,1,0:T(8,128)(2,1)} %copy.47, pred[16,2,6]{2,1,0:T(4,128)(4,1)S(1)} %compare_and_fusion, pred[16,2,6]{2,1,0:T(4,128)(4,1)S(1)} %iota_compare_fusion.1, ...), kind=kOutput, calls=%fused_computation.102 | convolution fusion | flops 3253731328 | bytes 44061056 | tf_op jit(solution)/shard_map/bamij,bamjk->baik/dot_general | solution.py:54
  163.3 9.7 %exponential_reduce_fusion = f32[16,128,512]{1,2,0:T(8,128)} fusion(f32[16,2,128,512]{2,3,1,0:T(8,128)S(1)} %get-tuple-element.17, f32[16,128,512]{1,2,0:T(8,128)} %get-tuple-element.16), kind=kLoop, calls=%fused_computation.16 | loop fusion | flops 3145728 | bytes 16777216 | tf_op jit(solution)/shard_map/reduce_sum | solution.py:60
  173.1 6.0 %log_add_fusion = f32[16,128,512]{1,2,0:T(8,128)} fusion(f32[16,128,512]{1,2,0:T(8,128)} %get-tuple-element.16, f32[16,128,512]{1,2,0:T(8,128)} %exponential_reduce_fusion), kind=kLoop, calls=%fused_computation.26 | loop fusion | flops 1048576 | bytes 12582912 | tf_op jit(solution)/shard_map/add | solution.py:60
  179.1 24.5 %fusion.10 = f32[16,2,512,6,128]{4,2,3,1,0:T(8,128)} fusion(bf16[16,2,6,128,128]{4,3,2,1,0:T(8,128)(2,1)} %param.11, f32[16,2,128,512]{2,3,1,0:T(8,128)} %copy-done, f32[16,128,512]{1,2,0:T(8,128)} %log_add_fusion, f32[16,128,512]{1,2,0:T(8,128)} %copy.49), kind=kOutput, calls=%fused_computation.22 | convolution fusion | flops 3229614080 | bytes 73400320 | tf_op jit(solution)/shard_map/bamij,baik->bamjk/dot_general | solution.py:73
  203.6 4.5 %gather_fusion.2 = bf16[24,128,512]{1,2,0:T(8,128)(2,1)S(1)} fusion(f32[192,128,512]{1,2,0:T(8,128)} %bitcast.71, s32[1024]{0:T(1024)S(1)} %pad_clamp_fusion), kind=kCustom, calls=%fused_computation.2 | custom fusion | bytes 6291552 | tf_op jit(solution)/shard_map/jit(_take)/gather | solution.py:77
  208.1 2.8 copy.51
  210.8 5.0 %select_convert_fusion = bf16[4,6,128,512]{3,2,1,0:T(8,128)(2,1)} fusion(bf16[4,6,128,512]{3,2,1,0:T(8,128)(2,1)} %bitcast.78, pred[4,6]{1,0:T(4,128)(4,1)S(1)} %broadcast_in_dim.91, pred[4,6]{1,0:T(4,128)(4,1)S(1)} %broadcast_in_dim.89), kind=kLoop, calls=%fused_computation.17 | loop fusion | flops 3145728 | bytes 6291504 | tf_op jit(solution)/shard_map/convert_element_type | solution.py:78
  215.8 3.7 %all-to-all-start.2 = ((bf16[4,6,128,512]{3,2,1,0:T(8,128)(2,1)}), bf16[4,6,128,512]{3,2,1,0:T(8,128)(2,1)S(1)}, u32[]{:S(2)}, u32[]{:S(2)}) async-start(bf16[4,6,128,512]{3,2,1,0:T(8,128)(2,1)} %select_convert_fusion), calls=%async_computation.2 | async-start | bytes 6291456 | tf_op jit(solution)/shard_map/all_to_all | solution.py:79
  219.5 0.1 reshape.399
  219.6 5.3 %copy.48 = f32[16,128,512]{2,1,0:T(8,128)} copy(f32[16,128,512]{1,2,0:T(8,128)} %log_add_fusion) | data formatting | bytes 8388608 | tf_op jit(solution)/shard_map/add | solution.py:60
  225.0 49.2 %copy.50 = f32[192,128,512]{2,0,1:T(8,128)} copy(f32[192,128,512]{1,2,0:T(8,128)} %bitcast.72) | data formatting | bytes 100663296 | tf_op jit(solution)/shard_map/reshape | solution.py:75
  274.2 7.5 %fusion.7 = (f32[2,512]{1,0:T(2,128)S(1)}, f32[16,2,128]{2,1,0:T(2,128)S(1)}) fusion(f32[16,2,128,512]{2,3,1,0:T(8,128)} %copy-done, f32[16,128,512]{1,2,0:T(8,128)} %log_add_fusion, f32[16,128,512]{1,2,0:T(8,128)} %copy.49), kind=kLoop, calls=%fused_computation.18 | loop fusion | flops 8383488 | bytes 16797696 | tf_op jit(solution)/shard_map/reduce_sum | solution.py:67
  281.7 12.2 %psum.15 = f32[2,512]{1,0:T(2,128)S(1)} all-reduce(f32[2,512]{1,0:T(2,128)S(1)} %get-tuple-element.4), channel_id=1, replica_groups=mesh['groups'=2,'state'=4,'type'=4] {'state'}, use_global_device_ids=true, to_apply=%region_10.11 | all-reduce | flops 1024 | bytes 8192 | tf_op jit(solution)/shard_map/psum | solution.py:67
  293.8 10.1 %psum.14 = f32[2,2048]{1,0:T(2,128)S(1)} all-reduce(f32[2,2048]{1,0:T(2,128)S(1)} %bitcast.82), channel_id=1, replica_groups=mesh['groups'=2,'state'=4,'type'=4] {'type'}, use_global_device_ids=true, to_apply=%region_8.9 | all-reduce | flops 4096 | bytes 32768 | tf_op jit(solution)/shard_map/psum | solution.py:66
  303.9 0.6 broadcast_multiply_fusion.1
  304.5 0.6 broadcast_multiply_fusion
  305.1 23.2 %fusion.26 = f32[16,128,512]{2,0,1:T(8,128)} fusion(f32[192,128,512]{2,0,1:T(8,128)} %copy.50, s32[192]{0:T(256)S(1)} %and_select_fusion.4, pred[192]{0:T(512)(128)(4,1)S(1)} %get-tuple-element.10), kind=kOutput, calls=%fused_computation.45 | convolution fusion | flops 2415925248 | bytes 54526912 | tf_op jit(solution)/shard_map/rd,rjk->djk/dot_general | solution.py:90
  328.4 5.1 %fusion.20 = f32[16,128,512]{2,0,1:T(8,128)S(1)} fusion(f32[16,128,512]{2,0,1:T(8,128)} %fusion.26, s32[24]{0:T(128)S(1)} %reshape.399, bf16[3,8,128,512]{3,2,1,0:T(8,128)(2,1)S(1)} %bitcast.77), kind=kOutput, calls=%fused_computation.31 | convolution fusion | flops 51380608 | bytes 11534432 | tf_op jit(solution)/shard_map/dot_general | solution.py:92
  333.4 4.4 %copy.53 = f32[16,128,512]{2,1,0:T(8,128)} copy(f32[16,128,512]{2,0,1:T(8,128)S(1)} %fusion.20) | data formatting | bytes 8388608 | tf_op jit(solution)/shard_map/add | solution.py:97
  (30 shorter events, 0.4 us)
Async XLA Ops:
  23.2 74.4 %copy-start.1 = (bf16[2048,512]{1,0:T(8,128)(2,1)S(1)}, bf16[2048,512]{1,0:T(8,128)(2,1)}, u32[]{:S(2)}) copy-start(bf16[2048,512]{1,0:T(8,128)(2,1)} %param.7) | copy-start | bytes 6291460
  23.2 74.4 %all-to-all-start.1 = ((bf16[4,6,128,512]{3,2,1,0:T(8,128)(2,1)}), bf16[4,6,128,512]{3,2,1,0:T(8,128)(2,1)}, u32[]{:S(2)}, u32[]{:S(2)}) async-start(bf16[4,6,128,512]{3,2,1,0:T(8,128)(2,1)} %broadcast_select_fusion), calls=%async_computation.1 | async-start | bytes 6291456 | tf_op jit(solution)/shard_map/all_to_all | solution.py:40
  115.8 32.6 %copy-start.2 = (f32[2,2048]{1,0:T(2,128)S(1)}, f32[2,2048]{1,0:T(2,128)}, u32[]{:S(2)}) copy-start(f32[2,2048]{1,0:T(2,128)} %param.9) | copy-start | bytes 49156
  115.8 32.6 %copy-start.3 = (f32[2,512]{1,0:T(2,128)S(1)}, f32[2,512]{1,0:T(2,128)}, u32[]{:S(2)}) copy-start(f32[2,512]{1,0:T(2,128)} %param.10) | copy-start | bytes 12292
  163.3 9.7 %copy-start = (f32[16,2,128,512]{2,3,1,0:T(8,128)}, f32[16,2,128,512]{2,3,1,0:T(8,128)S(1)}, u32[]{:S(2)}) copy-start(f32[16,2,128,512]{2,3,1,0:T(8,128)S(1)} %get-tuple-element.17) | copy-start | bytes 25165828
  215.8 112.5 %all-to-all-start.2 = ((bf16[4,6,128,512]{3,2,1,0:T(8,128)(2,1)}), bf16[4,6,128,512]{3,2,1,0:T(8,128)(2,1)S(1)}, u32[]{:S(2)}, u32[]{:S(2)}) async-start(bf16[4,6,128,512]{3,2,1,0:T(8,128)(2,1)} %select_convert_fusion), calls=%async_computation.2 | async-start | bytes 6291456 | tf_op jit(solution)/shard_map/all_to_all | solution.py:79
where the time goes:
time: 340 us; the launch traced here: 338 us
  local copies, waits for them, and re-layouts  125 us (37%)
  matrix products  67.8 us (20%)
  waiting for transfers between devices  63.7 us (19%)
  other arithmetic  38.5 us (11%)
  blocking collectives  34 us (10%)
  starting transfers between devices  8.47 us (2%)
    all_to_all x1, waiting for transfers between devices, local(): lax.all_to_all(outgoing.reshape(device_count, capacity, tile_rows, type_w...  63.7 us
    reshape x1, local copies, waits for them, and re-layouts, local(): contrib = jnp.einsum('bamij,baik->bamjk', tiles, scaled, preferred_elemen...  49.2 us
    gather x2, local copies, waits for them, and re-layouts, local(): picked = jnp.take(table, lookup, axis=0)  46.1 us
    dot_general x1, matrix products, local(): jnp.einsum('bamij,baik->bamjk', tiles, scaled, preferred_element_type=jnp...  24.5 us
    dot_general x1, matrix products, local(): jnp.einsum('rd,rjk->djk', local_select, contrib, precision=lax.Precision....  23.2 us
    dot_general x1, matrix products, local(): jnp.einsum('bamij,bamjk->baik', tiles, picked, preferred_element_type=jnp...  15 us
    psum x1, blocking collectives, local(): lax.psum(jnp.sum(grad_q, axis=(0, 2)), 'state')  12.2 us
    all_to_all x1, blocking collectives, local(): lax.all_to_all(request.reshape(device_count, capacity), 'state', split_ax...  11.7 us
  transfers between devices with their start and end apart: 2, of which 1 were waited for; matrix products, arithmetic and copies ran while one was open for 27% of the time, Pallas kernels for 0%

commit v1 on v0

v1 whole, which is shorter than its diff:
```python
import functools

import jax
import jax.numpy as jnp
from jax import lax
from jax.experimental import pallas as pl
from jax.experimental.pallas import tpu as pltpu
from jax.sharding import PartitionSpec as P

VMEM = pltpu.VMEM
SMEM = pltpu.SMEM
MESH = pl.DeviceIdType.MESH


def smem():
    return pl.BlockSpec(memory_space=SMEM)


def whole(shape):
    return pl.BlockSpec(shape, lambda *g: (0,) * len(shape))


def plan_kernel(dims, me_ref, dest_ref, count_ref, req_ref, look_ref, start_ref, act_ref, pos_ref, slot_ref, fill):
    B, A, M, D, cap = dims
    me = me_ref[0]

    def clear(p, carry):
        fill[p] = 0
        for s in range(cap):
            req_ref[p, 0, s] = -1
        return carry

    lax.fori_loop(0, D, clear, 0)

    def lists(i, total):
        start_ref[i] = total
        for a in range(A):
            count = count_ref[i * A + a]
            for n in range(M):
                e = (i * A + a) * M + n
                dest = dest_ref[e]
                owner = lax.div(dest, B)
                block = dest - owner * B
                used = n < count
                look_ref[e] = jnp.where(used & (owner == me), block, -1)
                far = used & (owner != me)

                @pl.when(far)
                def _():
                    s = fill[owner]
                    req_ref[owner, 0, s] = block
                    fill[owner] = s + 1
                    act_ref[total] = a
                    pos_ref[total] = n
                    slot_ref[total] = owner * cap + s

                total = total + far.astype(jnp.int32)
        return total

    start_ref[B] = lax.fori_loop(0, B, lists, 0)


def greet(axis, others):
    barrier = pltpu.get_barrier_semaphore()
    for ids in others:
        pl.semaphore_signal(barrier, inc=1, device_id=ids, device_id_type=MESH)
    pl.semaphore_wait(barrier, len(others))


def request_kernel(D, req_ref, out_ref, land, send, recv):
    me = lax.axis_index("state")
    peers = [{"state": lax.rem(me + k, D)} for k in range(1, D)]
    greet("state", peers)
    copies = []
    for k in range(1, D):
        c = pltpu.make_async_remote_copy(
            src_ref=req_ref.at[lax.rem(me + k, D)],
            dst_ref=land.at[k],
            send_sem=send.at[k],
            recv_sem=recv.at[k],
            device_id={"state": lax.rem(me + k, D)},
            device_id_type=MESH,
        )
        c.start()
        copies.append(c)
    for c in copies:
        c.wait()
    out_ref[me] = req_ref[me]
    for k in range(1, D):
        out_ref[lax.rem(me - k + D, D)] = land[k]


def gather_kernel(D, cap, want_ref, val_ref, out_ref, sem):
    def copy(p, s):
        w = jnp.maximum(want_ref[p, 0, s], 0)
        return pltpu.make_async_copy(val_ref.at[w], out_ref.at[p * cap + s], sem.at[p * cap + s])

    def start(p, carry):
        for s in range(cap):
            copy(p, s).start()
        return carry

    def wait(p, carry):
        for s in range(cap):
            copy(p, s).wait()
        return carry

    lax.fori_loop(0, D, start, 0)
    lax.fori_loop(0, D, wait, 0)


def near_kernel(A, M, look_ref, val_ref, tiles_ref, cont_ref):
    i = pl.program_id(0)
    for a in range(A):
        weights, values = [], []
        for n in range(M):
            block = look_ref[(i * A + a) * M + n]
            keep = jnp.where(block >= 0, 1.0, 0.0).astype(jnp.float32)
            tile = tiles_ref[0, a, n]
            weights.append(tile * jnp.full(tile.shape, keep, jnp.float32).astype(jnp.bfloat16))
            values.append(val_ref[jnp.maximum(block, 0)])
        cont_ref[0, a] = jnp.dot(
            jnp.concatenate(weights, axis=1),
            jnp.concatenate(values, axis=0),
            preferred_element_type=jnp.float32,
        )


def transposed_dot(tile, right):
    return lax.dot_general(tile, right, (((0,), (0,)), ((), ())), preferred_element_type=jnp.float32)


def value_kernel(
    rows, start_ref, act_ref, pos_ref, slot_ref, cont_ref, inc_ref, tiles_ref, cot_ref, util_ref, taste_ref,
    value_ref, scaled_ref, out_ref, gu_ref, gt_ref, acc,
):
    i = pl.program_id(0)
    first, last = start_ref[i], start_ref[i + 1]
    acc[...] = cont_ref[0]

    def far(r, carry):
        a = act_ref[r]
        acc[a] += jnp.dot(
            tiles_ref[0, a, pos_ref[r]], inc_ref[slot_ref[r]], preferred_element_type=jnp.float32
        )
        return carry

    lax.fori_loop(first, last, far, 0)

    @pl.when(i == 0)
    def _():
        gt_ref[...] = jnp.zeros_like(gt_ref)

    tile_rows, width = cot_ref.shape
    t0, t1 = taste_ref[0:1, :], taste_ref[1:2, :]

    def chunk(c, carry):
        g0, g1 = carry
        at = pl.ds(pl.multiple_of(c * rows, rows), rows)
        util = util_ref[0, at, :]
        q0 = util[:, 0:1] + t0 + 0.95 * acc[0, at, :]
        q1 = util[:, 1:2] + t1 + 0.95 * acc[1, at, :]
        gap = q1 - q0
        small = jnp.exp(-jnp.abs(gap))
        total = 1.0 + small
        value_ref[at, :] = jnp.maximum(q0, q1) + jnp.log(total)
        big = cot_ref[at, :].astype(jnp.float32) / total
        little = big * small
        first_wins = gap <= 0.0
        h0 = jnp.where(first_wins, big, little)
        h1 = jnp.where(first_wins, little, big)
        scaled_ref[0, 0, at, :] = (0.95 * h0).astype(jnp.bfloat16)
        scaled_ref[0, 1, at, :] = (0.95 * h1).astype(jnp.bfloat16)
        gu_ref[0, at, 0:1] = jnp.sum(h0, axis=1, keepdims=True)
        gu_ref[0, at, 1:2] = jnp.sum(h1, axis=1, keepdims=True)
        return g0 + h0, g1 + h1

    zero = jnp.zeros((rows, width), jnp.float32)
    g0, g1 = lax.fori_loop(0, tile_rows // rows, chunk, (zero, zero))
    gt_ref[0:1, :] += jnp.sum(g0, axis=0, keepdims=True)
    gt_ref[1:2, :] += jnp.sum(g1, axis=0, keepdims=True)

    def back(r, carry):
        a = act_ref[r]
        out_ref[slot_ref[r]] = transposed_dot(tiles_ref[0, a, pos_ref[r]], scaled_ref[0, a]).astype(jnp.bfloat16)
        return carry

    lax.fori_loop(first, last, back, 0)


def back_kernel(A, M, look_ref, tiles_ref, scaled_ref, adj_ref):
    i = pl.program_id(0)

    @pl.when(i == 0)
    def _():
        adj_ref[...] = jnp.zeros_like(adj_ref)

    for a in range(A):
        for n in range(M):
            block = look_ref[(i * A + a) * M + n]

            @pl.when(block >= 0)
            def _():
                adj_ref[block] += transposed_dot(tiles_ref[0, a, n], scaled_ref[0, a])


def sums_kernel(D, T, gu_ref, gt_ref, ou_ref, ot_ref, lu, lt, us, ur, ts, tr):
    ms, mt = lax.axis_index("state"), lax.axis_index("type")
    peers = [{"state": lax.rem(ms + k, D)} for k in range(1, D)]
    peers += [{"type": lax.rem(mt + k, T)} for k in range(1, T)]
    greet("state", peers)
    copies = []
    for k in range(1, T):
        copies.append(
            pltpu.make_async_remote_copy(
                src_ref=gu_ref, dst_ref=lu.at[k], send_sem=us.at[k], recv_sem=ur.at[k],
                device_id={"type": lax.rem(mt + k, T)}, device_id_type=MESH,
            )
        )
    for k in range(1, D):
        copies.append(
            pltpu.make_async_remote_copy(
                src_ref=gt_ref, dst_ref=lt.at[k], send_sem=ts.at[k], recv_sem=tr.at[k],
                device_id={"state": lax.rem(ms + k, D)}, device_id_type=MESH,
            )
        )
    for c in copies:
        c.start()
    for c in copies:
        c.wait()
    lu[0] = gu_ref[...]
    lt[0] = gt_ref[...]
    u = lu[lax.rem(mt, T)]
    for j in range(1, T):
        u = u + lu[lax.rem(mt - j + T, T)]
    t = lt[lax.rem(ms, D)]
    for j in range(1, D):
        t = t + lt[lax.rem(ms - j + D, D)]
    ou_ref[...] = u
    ot_ref[...] = t


def land_kernel(D, cap, want_ref, adj_ref, ret_ref, out_ref):
    j = pl.program_id(0)
    out_ref[...] = adj_ref[...]

    def peer(p, carry):
        for s in range(cap):

            @pl.when(want_ref[p, 0, s] == j)
            def _():
                out_ref[0] += ret_ref[p * cap + s].astype(jnp.float32)

        return carry

    lax.fori_loop(0, D, peer, 0)


def local(value_in, cotangent, state_util, taste, tiles, dest_block, counts):
    B, A, M, R, _ = tiles.shape
    W = value_in.shape[1]
    D = lax.axis_size("state")
    T = lax.axis_size("type")
    cap = max(2, (B + D - 2) // (D - 1))
    E, C = B * A * M, D * cap
    f32, bf16, i32 = jnp.float32, jnp.bfloat16, jnp.int32
    shape = jax.ShapeDtypeStruct
    values = value_in.reshape(B, R, W)

    req, look, start, act, pos, slot = pl.pallas_call(
        functools.partial(plan_kernel, (B, A, M, D, cap)),
        out_shape=(
            shape((D, 1, 128), i32), shape((E,), i32), shape((B + 1,), i32),
            shape((C,), i32), shape((C,), i32), shape((C,), i32),
        ),
        in_specs=[smem()] * 3,
        out_specs=[smem()] * 6,
        scratch_shapes=[SMEM((D,), i32)],
        name="plan",
    )(lax.axis_index("state").reshape(1).astype(i32), dest_block.reshape(E), counts.reshape(B * A))

    wanted = pl.pallas_call(
        functools.partial(request_kernel, D),
        out_shape=shape((D, 1, 128), i32),
        in_specs=[pl.BlockSpec(memory_space=VMEM)],
        out_specs=pl.BlockSpec(memory_space=VMEM),
        scratch_shapes=[VMEM((D, 1, 128), i32), pltpu.SemaphoreType.DMA((D,)), pltpu.SemaphoreType.DMA((D,))],
        compiler_params=pltpu.CompilerParams(collective_id=0, has_side_effects=True),
        name="request",
    )(req)

    outgoing = pl.pallas_call(
        functools.partial(gather_kernel, D, cap),
        out_shape=shape((C, R, W), bf16),
        in_specs=[smem(), pl.BlockSpec(memory_space=VMEM)],
        out_specs=pl.BlockSpec(memory_space=pl.ANY),
        scratch_shapes=[pltpu.SemaphoreType.DMA((C,))],
        name="gather",
    )(wanted, values)

    incoming = lax.all_to_all(
        outgoing.reshape(D, cap, R, W), "state", split_axis=0, concat_axis=0, tiled=True
    ).reshape(C, R, W)

    tile_spec = pl.BlockSpec((1, A, M, R, R), lambda i: (i, 0, 0, 0, 0))
    pair_spec = pl.BlockSpec((1, A, R, W), lambda i: (i, 0, 0, 0))
    row_spec = pl.BlockSpec((R, W), lambda i: (i, 0))
    flops = 2 * E * R * R * W

    cont = pl.pallas_call(
        functools.partial(near_kernel, A, M),
        grid=(B,),
        out_shape=shape((B, A, R, W), f32),
        in_specs=[smem(), whole((B, R, W)), tile_spec],
        out_specs=pair_spec,
        cost_estimate=pl.CostEstimate(flops=flops, bytes_accessed=16 << 20, transcendentals=0),
        name="near",
    )(look, values, tiles)

    util_cols = state_util.reshape(A, B, R).transpose(1, 2, 0)
    value, scaled, outbound, gu, gt = pl.pallas_call(
        functools.partial(value_kernel, 16),
        grid=(B,),
        out_shape=(
            shape((B * R, W), f32), shape((B, A, R, W), bf16), shape((C, R, W), bf16),
            shape((B, R, A), f32), shape((A, W), f32),
        ),
        in_specs=[smem()] * 4
        + [
            pair_spec, whole((C, R, W)), tile_spec, row_spec,
            pl.BlockSpec((1, R, A), lambda i: (i, 0, 0)), whole((A, W)),
        ],
        out_specs=[
            row_spec, pair_spec, whole((C, R, W)), pl.BlockSpec((1, R, A), lambda i: (i, 0, 0)), whole((A, W)),
        ],
        scratch_shapes=[VMEM((A, R, W), f32)],
        cost_estimate=pl.CostEstimate(flops=flops // 4, bytes_accessed=30 << 20, transcendentals=3 * B * R * W),
        name="value",
    )(start, act, pos, slot, cont, incoming, tiles, cotangent, util_cols, taste)

    returned = lax.all_to_all(
        outbound.reshape(D, cap, R, W), "state", split_axis=0, concat_axis=0, tiled=True
    ).reshape(C, R, W)

    adj = pl.pallas_call(
        functools.partial(back_kernel, A, M),
        grid=(B,),
        out_shape=shape((B, R, W), f32),
        in_specs=[smem(), tile_spec, pair_spec],
        out_specs=whole((B, R, W)),
        cost_estimate=pl.CostEstimate(flops=flops, bytes_accessed=14 << 20, transcendentals=0),
        name="back",
    )(look, tiles, scaled)

    gu_rows = gu.transpose(2, 0, 1).reshape(A, B * R) / (W * T)
    grad_util, grad_taste = pl.pallas_call(
        functools.partial(sums_kernel, D, T),
        out_shape=(shape((A, B * R), f32), shape((A, W), f32)),
        in_specs=[pl.BlockSpec(memory_space=VMEM)] * 2,
        out_specs=[pl.BlockSpec(memory_space=VMEM)] * 2,
        scratch_shapes=[
            VMEM((T, A, B * R), f32), VMEM((D, A, W), f32),
            pltpu.SemaphoreType.DMA((T,)), pltpu.SemaphoreType.DMA((T,)),
            pltpu.SemaphoreType.DMA((D,)), pltpu.SemaphoreType.DMA((D,)),
        ],
        compiler_params=pltpu.CompilerParams(collective_id=1, has_side_effects=True),
        cost_estimate=pl.CostEstimate(flops=0, bytes_accessed=8 << 20, transcendentals=0),
        name="sums",
    )(gu_rows, gt / (B * R * D))

    block_spec = pl.BlockSpec((1, R, W), lambda j: (j, 0, 0))
    adjoint = pl.pallas_call(
        functools.partial(land_kernel, D, cap),
        grid=(B,),
        out_shape=shape((B, R, W), f32),
        in_specs=[smem(), block_spec, whole((C, R, W))],
        out_specs=block_spec,
        name="land",
    )(wanted, adj, returned)
    return value, adjoint.reshape(B * R, W), grad_util, grad_taste


def solution(mesh):
    rows = ("groups", "state")
    return jax.shard_map(
        local,
        mesh=mesh,
        in_specs=(
            P(rows, "type"),
            P(rows, "type"),
            P(None, rows),
            P(None, ("groups", "type")),
            P(rows, None, None, None, None),
            P(rows, None, None),
            P(rows, None),
        ),
        out_specs=(P(rows, "type"), P(rows, "type"), P(None, rows), P(None, ("groups", "type"))),
        check_vma=False,
    )
```

time: 340 us -> 249 us (0.73)
  Pallas kernels: 0 us -> 172 us
  local copies, waits for them, and re-layouts: 125 us -> 10.9 us
  matrix products: 67.8 us -> 0 us
  other arithmetic: 38.5 us -> 2.91 us
  blocking collectives: 34 us -> 0 us
  waiting for transfers between devices: 63.7 us -> 53.2 us
    pallas_call x0 -> x8, Pallas kernels: none -> 172 us  [the longest x1 66.2 us: local(): pl.pallas_call(functools.partial(sums_kernel, D, T), out_shape=(shape((A,...]
    dot_general x4 -> x0, matrix products: 67.8 us -> none  [the longest x1 24.5 us: local(): jnp.einsum('bamij,baik->bamjk', tiles, scaled, preferred_element_type=jnp...]
    gather x5 -> x0, local copies, waits for them, and re-layouts: 55.7 us -> none  [the longest x2 46.1 us: local(): picked = jnp.take(table, lookup, axis=0)]
    reshape x4 -> x2, local copies, waits for them, and re-layouts: 49.5 us -> 1.28 us  [the longest x1 0.68 us: local(): dest_block.reshape(E)]
    psum x2 -> x0, blocking collectives: 22.3 us -> none  [the longest x1 12.2 us: local(): lax.psum(jnp.sum(grad_q, axis=(0, 2)), 'state')]
    reduce_sum x3 -> x0, other arithmetic: 17.2 us -> none  [the longest x1 9.72 us: local(): jnp.sum(jnp.exp(scores - largest[:, None]), axis=1)]
    all_to_all x1 -> x0, blocking collectives: 11.7 us -> none  [local(): lax.all_to_all(request.reshape(device_count, capacity), 'state', split_ax...]
    all_to_all x2, waiting for transfers between devices: 63.7 us -> 53.2 us  [the longest x1 53.2 us: local(): lax.all_to_all(outgoing.reshape(D, cap, R, W), 'state', split_axis=0, con...]
  transfers between devices with their start and end apart: 2 -> 2, of which waited for: 1 -> 1; matrix products, arithmetic and copies ran while one was open for 27% -> 3% of each run, Pallas kernels for 0% -> 43%
where the time goes in v1:
time: 249 us; the launch traced here: 248 us
  Pallas kernels  172 us (69%)
  waiting for transfers between devices  53.2 us (21%)
  local copies, waits for them, and re-layouts  10.9 us (4%)
  starting transfers between devices  8.26 us (3%)
  other arithmetic  2.91 us (1%)
    pallas_call x1, Pallas kernels, local(): pl.pallas_call(functools.partial(sums_kernel, D, T), out_shape=(shape((A,...  66.2 us
    all_to_all x1, waiting for transfers between devices, local(): lax.all_to_all(outgoing.reshape(D, cap, R, W), 'state', split_axis=0, con...  53.2 us
    pallas_call x1, Pallas kernels, local(): pl.pallas_call(functools.partial(value_kernel, 16), grid=(B,), out_shape=...  35.7 us
    pallas_call x1, Pallas kernels, local(): pl.pallas_call(functools.partial(back_kernel, A, M), grid=(B,), out_shape...  26.7 us
    pallas_call x1, Pallas kernels, local(): pl.pallas_call(functools.partial(near_kernel, A, M), grid=(B,), out_shape...  14.9 us
    pallas_call x1, Pallas kernels, local(): pl.pallas_call(functools.partial(land_kernel, D, cap), grid=(B,), out_sha...  13.1 us
    pallas_call x1, Pallas kernels, local(): pl.pallas_call(functools.partial(request_kernel, D), out_shape=shape((D,...  8.54 us
    unnamed x17, local copies, waits for them, and re-layouts  7.51 us
  transfers between devices with their start and end apart: 2, of which 1 were waited for; matrix products, arithmetic and copies ran while one was open for 3% of the time, Pallas kernels for 43%

profile of v1, /device:TPU:0, one launch (start us, length us, event | category | flops | bytes accessed | tf_op | source)
XLA Modules:
  0.0 248.4 jit_solution(17466330737154945689)
XLA Ops:
  0.6 0.8 copy.15
  1.4 0.6 reshape.43.count_ref
  2.0 0.8 copy.14
  2.8 0.7 reshape.42.dest_ref
  3.4 3.7 %plan.1 = (s32[4,1,128]{2,1,0:T(1,128)}, s32[192]{0:T(256)}, s32[17]{0:T(128)}, s32[24]{0:T(128)}, s32[24]{0:T(128)}, /*index=5*/s32[24]{0:T(128)}) custom-call(s32[1]{0:T(128)} %bitcast.me_ref, s32[192]{0:T(256)} %reshape.42.dest_ref, s32[32]{0:T(128)} %reshape.43.count_ref), custom_call_target="tpu_custom_call" | custom-call | tf_op jit(solution)/shard_map/plan/pallas_call | solution.py:270
  7.2 8.5 %request.1.want_ref = s32[4,1,128]{2,1,0:T(1,128)} custom-call(s32[4,1,128]{2,1,0:T(1,128)} %get-tuple-element.22.req_ref), custom_call_target="tpu_custom_call" | custom-call | tf_op jit(solution)/shard_map/request/pallas_call | solution.py:282
  15.7 3.5 %gather.1 = bf16[24,128,512]{2,1,0:T(8,128)(2,1)} custom-call(s32[4,1,128]{2,1,0:T(1,128)} %request.1.want_ref, bf16[16,128,512]{2,1,0:T(8,128)(2,1)} %bitcast.16), custom_call_target="tpu_custom_call" | custom-call | tf_op jit(solution)/shard_map/gather/pallas_call | solution.py:292
  19.2 0.0 copy-start.2
  19.2 4.5 %all-to-all-start = ((bf16[4,6,128,512]{3,2,1,0:T(8,128)(2,1)}), bf16[4,6,128,512]{3,2,1,0:T(8,128)(2,1)S(1)}, u32[]{:S(2)}, u32[]{:S(2)}) async-start(bf16[4,6,128,512]{3,2,1,0:T(8,128)(2,1)} %bitcast.14), calls=%async_computation | async-start | bytes 6291456 | tf_op jit(solution)/shard_map/all_to_all | solution.py:301
  23.8 0.0 copy-done.2
  23.8 1.4 copy.16
  25.1 14.9 %near.1.cont_ref = f32[16,2,128,512]{3,2,1,0:T(8,128)} custom-call(s32[192]{0:T(256)} %get-tuple-element.21.look_ref, bf16[16,128,512]{2,1,0:T(8,128)(2,1)} %bitcast.17, bf16[16,2,6,128,128]{4,3,2,1,0:T(8,128)(2,1)} %tiles_ref.5), custom_call_target="tpu_custom_call" | custom-call | flops 3221225472 | bytes 16777216 | tf_op jit(solution)/shard_map/near/pallas_call | solution.py:310
  40.1 53.2 %all-to-all-done = bf16[4,6,128,512]{3,2,1,0:T(8,128)(2,1)S(1)} async-done(((bf16[4,6,128,512]{3,2,1,0:T(8,128)(2,1)}), bf16[4,6,128,512]{3,2,1,0:T(8,128)(2,1)S(1)}, u32[]{:S(2)}, u32[]{:S(2)}) %all-to-all-start) | async-done | bytes 3145760 | tf_op jit(solution)/shard_map/all_to_all | solution.py:301
  93.3 0.0 copy-start
  93.3 1.7 copy-done
  95.0 35.7 %value.1 = (f32[2048,512]{1,0:T(8,128)}, bf16[16,2,128,512]{3,2,1,0:T(8,128)(2,1)}, bf16[24,128,512]{2,1,0:T(8,128)(2,1)}, f32[16,128,2]{2,1,0:T(8,128)}, f32[2,512]{1,0:T(2,128)}) custom-call(s32[17]{0:T(128)} %get-tuple-element.17.start_ref, s32[24]{0:T(128)} %get-tuple-element.18.act_ref, s32[24]{0:T(128)} %get-tuple-element.19.pos_ref, ...), custom_call_target="tpu_custom_call" | custom-call | flops 805306368 | bytes 31457280 | tf_op jit(solution)/shard_map/value/pallas_call | solution.py:321
  130.7 0.0 copy-start.4
  130.7 3.7 %all-to-all-start.1 = ((bf16[4,6,128,512]{3,2,1,0:T(8,128)(2,1)}), bf16[4,6,128,512]{3,2,1,0:T(8,128)(2,1)S(1)}, u32[]{:S(2)}, u32[]{:S(2)}) async-start(bf16[4,6,128,512]{3,2,1,0:T(8,128)(2,1)} %bitcast.21), calls=%async_computation.1 | async-start | bytes 6291456 | tf_op jit(solution)/shard_map/all_to_all | solution.py:341
  134.4 2.3 broadcast_multiply_fusion
  136.7 2.2 copy.18.gu_ref
  138.9 0.0 copy-done.4
  138.9 0.6 broadcast_multiply_fusion.1.gt_ref
  139.5 66.2 %sums.1 = (f32[2,2048]{1,0:T(2,128)}, f32[2,512]{1,0:T(2,128)}) custom-call(f32[2,2048]{1,0:T(2,128)} %copy.18.gu_ref, f32[2,512]{1,0:T(2,128)} %broadcast_multiply_fusion.1.gt_ref), custom_call_target="tpu_custom_call" | custom-call | bytes 8388608 | tf_op jit(solution)/shard_map/sums/pallas_call | solution.py:356
  205.7 26.7 %back.1.adj_ref = f32[16,128,512]{2,1,0:T(8,128)} custom-call(s32[192]{0:T(256)} %get-tuple-element.21.look_ref, bf16[16,2,6,128,128]{4,3,2,1,0:T(8,128)(2,1)} %tiles_ref.5, bf16[16,2,128,512]{3,2,1,0:T(8,128)(2,1)} %get-tuple-element.24.scaled_ref), custom_call_target="tpu_custom_call" | custom-call | flops 3221225472 | bytes 14680064 | tf_op jit(solution)/shard_map/back/pallas_call | solution.py:345
  232.4 0.0 all-to-all-done.1
  232.4 0.0 copy-start.1
  232.4 1.7 copy-done.1
  234.1 0.0 copy-start.3
  234.1 0.0 copy-start.5
  234.1 13.1 %land.1 = f32[16,128,512]{2,1,0:T(8,128)} custom-call(s32[4,1,128]{2,1,0:T(1,128)} %request.1.want_ref, f32[16,128,512]{2,1,0:T(8,128)} %back.1.adj_ref, bf16[24,128,512]{2,1,0:T(8,128)(2,1)} %bitcast.15), custom_call_target="tpu_custom_call" | custom-call | tf_op jit(solution)/shard_map/land/pallas_call | solution.py:372
  247.2 0.0 copy-done.3
  247.2 0.6 copy.21
  247.9 0.0 copy-done.5
  247.9 0.6 copy.22
Async XLA Ops:
  19.2 4.6 %copy-start.2 = (f32[2,2048]{1,0:T(2,128)S(1)}, f32[2,2048]{1,0:T(2,128)}, u32[]{:S(2)}) copy-start(f32[2,2048]{1,0:T(2,128)} %param.9) | copy-start | bytes 49156
  19.2 74.1 %all-to-all-start = ((bf16[4,6,128,512]{3,2,1,0:T(8,128)(2,1)}), bf16[4,6,128,512]{3,2,1,0:T(8,128)(2,1)S(1)}, u32[]{:S(2)}, u32[]{:S(2)}) async-start(bf16[4,6,128,512]{3,2,1,0:T(8,128)(2,1)} %bitcast.14), calls=%async_computation | async-start | bytes 6291456 | tf_op jit(solution)/shard_map/all_to_all | solution.py:301
  93.3 1.7 copy-start
  130.7 8.2 %copy-start.4 = (f32[2,512]{1,0:T(2,128)S(1)}, f32[2,512]{1,0:T(2,128)}, u32[]{:S(2)}) copy-start(f32[2,512]{1,0:T(2,128)} %get-tuple-element.27) | copy-start | bytes 12292
  130.7 101.7 %all-to-all-start.1 = ((bf16[4,6,128,512]{3,2,1,0:T(8,128)(2,1)}), bf16[4,6,128,512]{3,2,1,0:T(8,128)(2,1)S(1)}, u32[]{:S(2)}, u32[]{:S(2)}) async-start(bf16[4,6,128,512]{3,2,1,0:T(8,128)(2,1)} %bitcast.21), calls=%async_computation.1 | async-start | bytes 6291456 | tf_op jit(solution)/shard_map/all_to_all | solution.py:341
  232.4 1.7 copy-start.1
  234.1 13.2 %copy-start.3 = (f32[2,2048]{1,0:T(2,128)S(1)}, f32[2,2048]{1,0:T(2,128)}, u32[]{:S(2)}) copy-start(f32[2,2048]{1,0:T(2,128)} %get-tuple-element.36) | copy-start | bytes 49156
  234.1 13.8 %copy-start.5 = (f32[2,512]{1,0:T(2,128)S(1)}, f32[2,512]{1,0:T(2,128)}, u32[]{:S(2)}) copy-start(f32[2,512]{1,0:T(2,128)} %get-tuple-element.37) | copy-start | bytes 12292

commit v2 on v1

v2 whole, which is shorter than its diff:
```python
import functools

import jax
import jax.numpy as jnp
from jax import lax
from jax.experimental import pallas as pl
from jax.experimental.pallas import tpu as pltpu
from jax.sharding import PartitionSpec as P

VMEM = pltpu.VMEM
SMEM = pltpu.SMEM
MESH = pl.DeviceIdType.MESH


def smem():
    return pl.BlockSpec(memory_space=SMEM)


def whole(shape):
    return pl.BlockSpec(shape, lambda *g: (0,) * len(shape))


def plan_kernel(dims, me_ref, dest_ref, count_ref, req_ref, look_ref, start_ref, act_ref, pos_ref, slot_ref, fill):
    B, A, M, D, cap = dims
    me = me_ref[0]

    def clear(p, carry):
        fill[p] = 0
        for s in range(cap):
            req_ref[p, 0, s] = -1
        return carry

    lax.fori_loop(0, D, clear, 0)

    def lists(i, total):
        start_ref[i] = total
        for a in range(A):
            count = count_ref[a, i]
            for n in range(M):
                e = (i * A + a) * M + n
                dest = dest_ref[n, a, i]
                owner = lax.div(dest, B)
                block = dest - owner * B
                used = n < count
                look_ref[e] = jnp.where(used & (owner == me), block, -1)
                far = used & (owner != me)

                @pl.when(far)
                def _():
                    s = fill[owner]
                    req_ref[owner, 0, s] = block
                    fill[owner] = s + 1
                    act_ref[total] = a
                    pos_ref[total] = n
                    slot_ref[total] = owner * cap + s

                total = total + far.astype(jnp.int32)
        return total

    start_ref[B] = lax.fori_loop(0, B, lists, 0)


def greet(axis, others):
    barrier = pltpu.get_barrier_semaphore()
    for ids in others:
        pl.semaphore_signal(barrier, inc=1, device_id=ids, device_id_type=MESH)
    pl.semaphore_wait(barrier, len(others))


def request_kernel(D, req_ref, out_ref, land, send, recv):
    me = lax.axis_index("state")
    peers = [{"state": lax.rem(me + k, D)} for k in range(1, D)]
    greet("state", peers)
    copies = []
    for k in range(1, D):
        c = pltpu.make_async_remote_copy(
            src_ref=req_ref.at[lax.rem(me + k, D)],
            dst_ref=land.at[k],
            send_sem=send.at[k],
            recv_sem=recv.at[k],
            device_id={"state": lax.rem(me + k, D)},
            device_id_type=MESH,
        )
        c.start()
        copies.append(c)
    for c in copies:
        c.wait()
    out_ref[me] = req_ref[me]
    for k in range(1, D):
        out_ref[lax.rem(me - k + D, D)] = land[k]


def gather_kernel(D, cap, half, want_ref, val_ref, *rest):
    outs, sem = rest[:-1], rest[-1]

    def run(h, act):
        def peer(p, carry):
            for s in range(cap):
                w = jnp.maximum(want_ref[p, 0, s], 0)
                act(
                    pltpu.make_async_copy(
                        val_ref.at[w, :, pl.ds(h * half, half)],
                        outs[h].at[p * cap + s],
                        sem.at[h, p * cap + s],
                    )
                )
            return carry

        lax.fori_loop(0, D, peer, 0)

    for h in range(len(outs)):
        run(h, lambda c: c.start())
    for h in range(len(outs)):
        run(h, lambda c: c.wait())


def near_kernel(G, A, M, look_ref, val_ref, tiles_ref, cont_ref):
    for g in range(G):
        i = pl.program_id(0) * G + g
        for a in range(A):
            weights, values = [], []
            for n in range(M):
                block = look_ref[(i * A + a) * M + n]
                keep = jnp.where(block >= 0, 1.0, 0.0).astype(jnp.float32)
                tile = tiles_ref[g, a, n]
                weights.append(tile * jnp.full(tile.shape, keep, jnp.float32).astype(jnp.bfloat16))
                values.append(val_ref[jnp.maximum(block, 0)])
            cont_ref[g, a] = jnp.dot(
                jnp.concatenate(weights, axis=1),
                jnp.concatenate(values, axis=0),
                preferred_element_type=jnp.float32,
            )


def transposed_dot(tile, right):
    return lax.dot_general(tile, right, (((0,), (0,)), ((), ())), preferred_element_type=jnp.float32)


def value_kernel(
    G, rows, start_ref, act_ref, pos_ref, slot_ref, cont_ref, inc_ref, tiles_ref, cot_ref, util_ref, taste_ref, *rest
):
    value_ref, scaled_ref, out_ref, gu_ref, gt_ref, acc = rest[-6:]
    step = pl.program_id(0)

    @pl.when(step == 0)
    def _():
        gt_ref[...] = jnp.zeros_like(gt_ref)

    R = tiles_ref.shape[3]
    acc[...] = cont_ref[...]
    t0, t1 = taste_ref[0:1, :], taste_ref[1:2, :]
    for g in range(G):
        i = step * G + g

        def far(r, carry):
            a = act_ref[r]
            acc[g, a] += jnp.dot(
                tiles_ref[g, a, pos_ref[r]], inc_ref[slot_ref[r]], preferred_element_type=jnp.float32
            )
            return carry

        lax.fori_loop(start_ref[i], start_ref[i + 1], far, 0)
    for g in range(G):
        g0 = g1 = 0.0
        for c in range(0, R, rows):
            at = slice(c, c + rows)
            here = slice(g * R + c, g * R + c + rows)
            util = util_ref[g, at, :]
            q0 = util[:, 0:1] + t0 + 0.95 * acc[g, 0, at, :]
            q1 = util[:, 1:2] + t1 + 0.95 * acc[g, 1, at, :]
            gap = q1 - q0
            small = jnp.exp(-jnp.abs(gap))
            total = 1.0 + small
            value_ref[here, :] = jnp.maximum(q0, q1) + jnp.log(total)
            big = cot_ref[here, :].astype(jnp.float32) / total
            little = big * small
            first_wins = gap <= 0.0
            h0 = jnp.where(first_wins, big, little)
            h1 = jnp.where(first_wins, little, big)
            scaled_ref[g, 0, at, :] = (0.95 * h0).astype(jnp.bfloat16)
            scaled_ref[g, 1, at, :] = (0.95 * h1).astype(jnp.bfloat16)
            gu_ref[g, at, 0:1] = jnp.sum(h0, axis=1, keepdims=True)
            gu_ref[g, at, 1:2] = jnp.sum(h1, axis=1, keepdims=True)
            g0, g1 = g0 + h0, g1 + h1
        gt_ref[0:1, :] += jnp.sum(g0, axis=0, keepdims=True)
        gt_ref[1:2, :] += jnp.sum(g1, axis=0, keepdims=True)
    for g in range(G):
        i = step * G + g

        def back(r, carry):
            a = act_ref[r]
            out_ref[slot_ref[r]] = transposed_dot(tiles_ref[g, a, pos_ref[r]], scaled_ref[g, a]).astype(jnp.bfloat16)
            return carry

        lax.fori_loop(start_ref[i], start_ref[i + 1], back, 0)


def back_kernel(G, A, M, look_ref, tiles_ref, scaled_ref, adj_ref):
    step = pl.program_id(0)

    @pl.when(step == 0)
    def _():
        adj_ref[...] = jnp.zeros_like(adj_ref)

    for g in range(G):
        i = step * G + g
        for a in range(A):
            for n in range(M):
                block = look_ref[(i * A + a) * M + n]

                @pl.when(block >= 0)
                def _():
                    adj_ref[block] += transposed_dot(tiles_ref[g, a, n], scaled_ref[g, a])


def sums_kernel(D, T, gu_ref, gt_ref, after_ref, ou_ref, ot_ref, lu, lt, us, ur, ts, tr):
    ms, mt = lax.axis_index("state"), lax.axis_index("type")
    peers = [{"state": lax.rem(ms + k, D)} for k in range(1, D)]
    peers += [{"type": lax.rem(mt + k, T)} for k in range(1, T)]
    greet("state", peers)
    copies = []
    for k in range(1, T):
        copies.append(
            pltpu.make_async_remote_copy(
                src_ref=gu_ref, dst_ref=lu.at[k], send_sem=us.at[k], recv_sem=ur.at[k],
                device_id={"type": lax.rem(mt + k, T)}, device_id_type=MESH,
            )
        )
    for k in range(1, D):
        copies.append(
            pltpu.make_async_remote_copy(
                src_ref=gt_ref, dst_ref=lt.at[k], send_sem=ts.at[k], recv_sem=tr.at[k],
                device_id={"state": lax.rem(ms + k, D)}, device_id_type=MESH,
            )
        )
    for c in copies:
        c.start()
    for c in copies:
        c.wait()
    lu[0] = gu_ref[...]
    lt[0] = gt_ref[...]
    u = lu[lax.rem(mt, T)]
    for j in range(1, T):
        u = u + lu[lax.rem(mt - j + T, T)]
    t = lt[lax.rem(ms, D)]
    for j in range(1, D):
        t = t + lt[lax.rem(ms - j + D, D)]
    ou_ref[...] = u
    ot_ref[...] = t


def land_kernel(D, cap, want_ref, adj_ref, ret_ref, *rest):
    out_ref = rest[-1]
    out_ref[...] = adj_ref[...]

    def peer(p, carry):
        for s in range(cap):
            w = want_ref[p, 0, s]

            @pl.when(w >= 0)
            def _():
                out_ref[w] += ret_ref[p * cap + s].astype(jnp.float32)

        return carry

    lax.fori_loop(0, D, peer, 0)


def local(value_in, cotangent, state_util, taste, tiles, dest_block, counts):
    B, A, M, R, _ = tiles.shape
    W = value_in.shape[1]
    D = lax.axis_size("state")
    T = lax.axis_size("type")
    cap = max(2, (B + D - 2) // (D - 1))
    E, C = B * A * M, D * cap
    f32, bf16, i32 = jnp.float32, jnp.bfloat16, jnp.int32
    shape = jax.ShapeDtypeStruct
    values = value_in.reshape(B, R, W)

    req, look, start, act, pos, slot = pl.pallas_call(
        functools.partial(plan_kernel, (B, A, M, D, cap)),
        out_shape=(
            shape((D, 1, 128), i32), shape((E,), i32), shape((B + 1,), i32),
            shape((C,), i32), shape((C,), i32), shape((C,), i32),
        ),
        in_specs=[smem()] * 3,
        out_specs=[smem()] * 6,
        scratch_shapes=[SMEM((D,), i32)],
        name="plan",
    )(lax.axis_index("state").reshape(1).astype(i32), dest_block.transpose(2, 1, 0), counts.T)

    wanted = pl.pallas_call(
        functools.partial(request_kernel, D),
        out_shape=shape((D, 1, 128), i32),
        in_specs=[pl.BlockSpec(memory_space=VMEM)],
        out_specs=pl.BlockSpec(memory_space=VMEM),
        scratch_shapes=[VMEM((D, 1, 128), i32), pltpu.SemaphoreType.DMA((D,)), pltpu.SemaphoreType.DMA((D,))],
        compiler_params=pltpu.CompilerParams(collective_id=0, has_side_effects=True),
        name="request",
    )(req)

    H = 2 if W % 256 == 0 else 1
    V = W // H
    G = 4 if B % 4 == 0 else 1
    outgoing = pl.pallas_call(
        functools.partial(gather_kernel, D, cap, V),
        out_shape=tuple(shape((C, R, V), bf16) for h in range(H)),
        in_specs=[smem(), pl.BlockSpec(memory_space=VMEM)],
        out_specs=[pl.BlockSpec(memory_space=pl.ANY)] * H,
        scratch_shapes=[pltpu.SemaphoreType.DMA((H, C))],
        name="gather",
    )(wanted, values)

    def exchange(x):
        return lax.all_to_all(
            x.reshape(D, cap, R, V), "state", split_axis=0, concat_axis=0, tiled=True
        ).reshape(C, R, V)

    incoming = [exchange(x) for x in outgoing]

    flops = 2 * E * R * R * W
    cont = pl.pallas_call(
        functools.partial(near_kernel, G, A, M),
        grid=(B // G,),
        out_shape=shape((B, A, R, W), f32),
        in_specs=[smem(), whole((B, R, W)), pl.BlockSpec((G, A, M, R, R), lambda i: (i, 0, 0, 0, 0))],
        out_specs=pl.BlockSpec((G, A, R, W), lambda i: (i, 0, 0, 0)),
        cost_estimate=pl.CostEstimate(flops=flops, bytes_accessed=16 << 20, transcendentals=0),
        name="near",
    )(look, values, tiles)

    util_cols = state_util.reshape(A, B, R).transpose(1, 2, 0)
    value = scaled = None
    gus, gts, outbound = [], [], []
    for h in range(H):
        held = [] if h == 0 else [value, scaled]
        value, scaled, out, gu, gt = pl.pallas_call(
            functools.partial(value_kernel, G, 32),
            grid=(B // G,),
            out_shape=(
                shape((B * R, W), f32), shape((B, A, R, W), bf16), shape((C, R, V), bf16),
                shape((B, R, A), f32), shape((A, V), f32),
            ),
            in_specs=[smem()] * 4
            + [
                pl.BlockSpec((G, A, R, V), lambda i, h=h: (i, 0, 0, h)),
                whole((C, R, V)),
                pl.BlockSpec((G, A, M, R, R), lambda i: (i, 0, 0, 0, 0)),
                pl.BlockSpec((G * R, V), lambda i, h=h: (i, h)),
                pl.BlockSpec((G, R, A), lambda i: (i, 0, 0)),
                pl.BlockSpec((A, V), lambda i, h=h: (0, h)),
            ]
            + [pl.BlockSpec(memory_space=pl.ANY)] * len(held),
            out_specs=[
                pl.BlockSpec((G * R, V), lambda i, h=h: (i, h)),
                pl.BlockSpec((G, A, R, V), lambda i, h=h: (i, 0, 0, h)),
                whole((C, R, V)),
                pl.BlockSpec((G, R, A), lambda i: (i, 0, 0)),
                whole((A, V)),
            ],
            input_output_aliases={10 + k: k for k in range(len(held))},
            scratch_shapes=[VMEM((G, A, R, V), f32)],
            cost_estimate=pl.CostEstimate(
                flops=flops // (4 * H), bytes_accessed=(30 << 20) // H, transcendentals=3 * B * R * V
            ),
            name="value",
        )(start, act, pos, slot, cont, incoming[h], tiles, cotangent, util_cols, taste, *held)
        outbound.append(out)
        gus.append(gu)
        gts.append(gt)

    returned = [exchange(x) for x in outbound]

    adj = pl.pallas_call(
        functools.partial(back_kernel, G, A, M),
        grid=(B // G,),
        out_shape=shape((B, R, W), f32),
        in_specs=[
            smem(),
            pl.BlockSpec((G, A, M, R, R), lambda i: (i, 0, 0, 0, 0)),
            pl.BlockSpec((G, A, R, W), lambda i: (i, 0, 0, 0)),
        ],
        out_specs=whole((B, R, W)),
        cost_estimate=pl.CostEstimate(flops=flops, bytes_accessed=14 << 20, transcendentals=0),
        name="back",
    )(look, tiles, scaled)

    gu_rows = sum(gus).transpose(2, 0, 1).reshape(A, B * R) / (W * T)
    grad_util, grad_taste = pl.pallas_call(
        functools.partial(sums_kernel, D, T),
        out_shape=(shape((A, B * R), f32), shape((A, W), f32)),
        in_specs=[pl.BlockSpec(memory_space=VMEM)] * 2 + [pl.BlockSpec(memory_space=pl.ANY)],
        out_specs=[pl.BlockSpec(memory_space=VMEM)] * 2,
        scratch_shapes=[
            VMEM((T, A, B * R), f32), VMEM((D, A, W), f32),
            pltpu.SemaphoreType.DMA((T,)), pltpu.SemaphoreType.DMA((T,)),
            pltpu.SemaphoreType.DMA((D,)), pltpu.SemaphoreType.DMA((D,)),
        ],
        compiler_params=pltpu.CompilerParams(collective_id=1, has_side_effects=True),
        cost_estimate=pl.CostEstimate(flops=0, bytes_accessed=8 << 20, transcendentals=0),
        name="sums",
    )(gu_rows, jnp.concatenate(gts, axis=1) / (B * R * D), adj)

    adjoint = adj
    for h in range(H):
        adjoint = pl.pallas_call(
            functools.partial(land_kernel, D, cap),
            grid=(1,),
            out_shape=shape((B, R, W), f32),
            in_specs=[smem(), pl.BlockSpec((B, R, V), lambda j, h=h: (0, 0, h)), whole((C, R, V))],
            out_specs=pl.BlockSpec((B, R, V), lambda j, h=h: (0, 0, h)),
            input_output_aliases={1: 0},
            name="land",
        )(wanted, adjoint, returned[h])
    return value, adjoint.reshape(B * R, W), grad_util, grad_taste


def solution(mesh):
    rows = ("groups", "state")
    return jax.shard_map(
        local,
        mesh=mesh,
        in_specs=(
            P(rows, "type"),
            P(rows, "type"),
            P(None, rows),
            P(None, ("groups", "type")),
            P(rows, None, None, None, None),
            P(rows, None, None),
            P(rows, None),
        ),
        out_specs=(P(rows, "type"), P(rows, "type"), P(None, rows), P(None, ("groups", "type"))),
        check_vma=False,
    )
```

time: 249 us -> 194 us (0.78)
  Pallas kernels: 172 us -> 107 us
  blocking collectives: 0 us -> 40.5 us
  waiting for transfers between devices: 53.2 us -> 26.8 us
  local copies, waits for them, and re-layouts: 10.9 us -> 5.93 us
  starting transfers between devices: 8.26 us -> 10.8 us
    pallas_call x1, Pallas kernels: 66.2 us -> 13.7 us  [local(): pl.pallas_call(functools.partial(sums_kernel, D, T), out_shape=(shape((A,...]
    all_to_all x0 -> x1, blocking collectives: none -> 40.5 us  [exchange(): lax.all_to_all(x.reshape(D, cap, R, V), 'state', split_axis=0, concat_axi...]
    all_to_all x2 -> x3, waiting for transfers between devices: 53.2 us -> 26.8 us  [exchange(): lax.all_to_all(x.reshape(D, cap, R, V), 'state', split_axis=0, concat_axi...]
    pallas_call x5 -> x7, Pallas kernels: 93.9 us -> 80.8 us  [the longest x2 35.3 us: local(): pl.pallas_call(functools.partial(value_kernel, G, 32), grid=(B // G,), ou...]
    unnamed x17 -> x19, local copies, waits for them, and re-layouts: 7.51 us -> 3.77 us
    all_to_all x2 -> x3, starting transfers between devices: 8.26 us -> 10.8 us  [exchange(): lax.all_to_all(x.reshape(D, cap, R, V), 'state', split_axis=0, concat_axi...]
  transfers between devices with their start and end apart: 2 -> 3, of which waited for: 1 -> 2; matrix products, arithmetic and copies ran while one was open for 3% -> 3% of each run, Pallas kernels for 43% -> 45%
where the time goes in v2:
time: 194 us; the launch traced here: 195 us
  Pallas kernels  107 us (55%)
  blocking collectives  40.5 us (21%)
  waiting for transfers between devices  26.8 us (14%)
  starting transfers between devices  10.8 us (6%)
  local copies, waits for them, and re-layouts  5.93 us (3%)
  other arithmetic  3.24 us (2%)
    all_to_all x1, blocking collectives, exchange(): lax.all_to_all(x.reshape(D, cap, R, V), 'state', split_axis=0, concat_axi...  40.5 us
    pallas_call x2, Pallas kernels, local(): pl.pallas_call(functools.partial(value_kernel, G, 32), grid=(B // G,), ou...  35.3 us
    all_to_all x3, waiting for transfers between devices, exchange(): lax.all_to_all(x.reshape(D, cap, R, V), 'state', split_axis=0, concat_axi...  26.8 us
    pallas_call x1, Pallas kernels, local(): pl.pallas_call(functools.partial(back_kernel, G, A, M), grid=(B // G,), o...  25 us
    pallas_call x1, Pallas kernels, local(): pl.pallas_call(functools.partial(sums_kernel, D, T), out_shape=(shape((A,...  13.7 us
    all_to_all x3, starting transfers between devices, exchange(): lax.all_to_all(x.reshape(D, cap, R, V), 'state', split_axis=0, concat_axi...  10.8 us
    pallas_call x1, Pallas kernels, local(): pl.pallas_call(functools.partial(near_kernel, G, A, M), grid=(B // G,), o...  9.06 us
    pallas_call x1, Pallas kernels, local(): pl.pallas_call(functools.partial(request_kernel, D), out_shape=shape((D,...  8.54 us
  transfers between devices with their start and end apart: 3, of which 2 were waited for; matrix products, arithmetic and copies ran while one was open for 3% of the time, Pallas kernels for 45%

profile of v2, /device:TPU:0, one launch (start us, length us, event | category | flops | bytes accessed | tf_op | source)
XLA Modules:
  0.0 195.0 jit_solution(5414356153228290967)
XLA Ops:
  0.6 3.9 %plan.1 = (s32[4,1,128]{2,1,0:T(1,128)}, s32[192]{0:T(256)}, s32[17]{0:T(128)}, s32[24]{0:T(128)}, s32[24]{0:T(128)}, /*index=5*/s32[24]{0:T(128)}) custom-call(s32[1]{0:T(128)} %bitcast.me_ref, s32[6,2,16]{2,1,0:T(2,128)} %bitcast.32, s32[2,16]{1,0:T(2,128)} %bitcast.33), custom_call_target="tpu_custom_call" | custom-call | tf_op jit(solution)/shard_map/plan/pallas_call | solution.py:280
  4.5 8.5 %request.1.want_ref = s32[4,1,128]{2,1,0:T(1,128)} custom-call(s32[4,1,128]{2,1,0:T(1,128)} %get-tuple-element.29.req_ref), custom_call_target="tpu_custom_call" | custom-call | tf_op jit(solution)/shard_map/request/pallas_call | solution.py:292
  13.1 3.7 %gather.1 = (bf16[24,128,256]{2,1,0:T(8,128)(2,1)}, bf16[24,128,256]{2,1,0:T(8,128)(2,1)}) custom-call(s32[4,1,128]{2,1,0:T(1,128)} %request.1.want_ref, bf16[16,128,512]{2,1,0:T(8,128)(2,1)} %bitcast.22), custom_call_target="tpu_custom_call" | custom-call | tf_op jit(solution)/shard_map/gather/pallas_call | solution.py:305
  16.8 40.5 %all_to_all.20 = bf16[4,6,128,256]{3,2,1,0:T(8,128)(2,1)} all-to-all(bf16[4,6,128,256]{3,2,1,0:T(8,128)(2,1)} %bitcast.31), channel_id=1, replica_groups=mesh['groups'=2,'state'=4,'type'=4] {'state'}, dimensions={0} | all-to-all | bytes 3145728 | tf_op jit(solution)/shard_map/all_to_all | solution.py:315
  57.3 0.0 copy-start.3
  57.3 3.7 %all-to-all-start = ((bf16[4,6,128,256]{3,2,1,0:T(8,128)(2,1)}), bf16[4,6,128,256]{3,2,1,0:T(8,128)(2,1)S(1)}, u32[]{:S(2)}, u32[]{:S(2)}) async-start(bf16[4,6,128,256]{3,2,1,0:T(8,128)(2,1)} %bitcast.4), calls=%async_computation | async-start | bytes 3145728 | tf_op jit(solution)/shard_map/all_to_all | solution.py:315
  61.0 0.0 copy-done.3
  61.0 1.4 copy.15
  62.4 9.1 %near.1.cont_ref = f32[16,2,128,512]{3,2,1,0:T(8,128)} custom-call(s32[192]{0:T(256)} %get-tuple-element.28.look_ref, bf16[16,128,512]{2,1,0:T(8,128)(2,1)} %bitcast.23, bf16[16,2,6,128,128]{4,3,2,1,0:T(8,128)(2,1)} %tiles_ref.7), custom_call_target="tpu_custom_call" | custom-call | flops 3221225472 | bytes 16777216 | tf_op jit(solution)/shard_map/near/pallas_call | solution.py:322
  71.4 17.6 %value.2 = (f32[2048,512]{1,0:T(8,128)}, bf16[16,2,128,512]{3,2,1,0:T(8,128)(2,1)}, bf16[24,128,256]{2,1,0:T(8,128)(2,1)}, f32[16,128,2]{2,1,0:T(8,128)}, f32[2,256]{1,0:T(2,128)}) custom-call(s32[17]{0:T(128)} %get-tuple-element.24.start_ref, s32[24]{0:T(128)} %get-tuple-element.25.act_ref, s32[24]{0:T(128)} %get-tuple-element.26.pos_ref, ...), custom_call_target="tpu_custom_call" | custom-call | flops 402653184 | bytes 15728640 | tf_op jit(solution)/shard_map/value/pallas_call | solution.py:337
  89.0 8.0 %all-to-all-done = bf16[4,6,128,256]{3,2,1,0:T(8,128)(2,1)S(1)} async-done(((bf16[4,6,128,256]{3,2,1,0:T(8,128)(2,1)}), bf16[4,6,128,256]{3,2,1,0:T(8,128)(2,1)S(1)}, u32[]{:S(2)}, u32[]{:S(2)}) %all-to-all-start) | async-done | bytes 1572896 | tf_op jit(solution)/shard_map/all_to_all | solution.py:315
  97.0 0.0 copy-start
  97.0 3.6 %all-to-all-start.2 = ((bf16[4,6,128,256]{3,2,1,0:T(8,128)(2,1)}), bf16[4,6,128,256]{3,2,1,0:T(8,128)(2,1)S(1)}, u32[]{:S(2)}, u32[]{:S(2)}) async-start(bf16[4,6,128,256]{3,2,1,0:T(8,128)(2,1)} %bitcast.30), calls=%async_computation.2 | async-start | bytes 3145728 | tf_op jit(solution)/shard_map/all_to_all | solution.py:315
  100.6 0.0 copy-done
  100.6 17.7 %value.3 = (f32[2048,512]{1,0:T(8,128)}, bf16[16,2,128,512]{3,2,1,0:T(8,128)(2,1)}, bf16[24,128,256]{2,1,0:T(8,128)(2,1)}, f32[16,128,2]{2,1,0:T(8,128)}, f32[2,256]{1,0:T(2,128)}) custom-call(s32[17]{0:T(128)} %get-tuple-element.24.start_ref, s32[24]{0:T(128)} %get-tuple-element.25.act_ref, ...), custom_call_target="tpu_custom_call", output_to_operand_aliasing={{0}: (10, {}), {1}: (11, {})} | custom-call | flops 402653184 | bytes 15728640 | tf_op jit(solution)/shard_map/value/pallas_call | solution.py:337
  118.3 18.8 %all-to-all-done.2 = bf16[4,6,128,256]{3,2,1,0:T(8,128)(2,1)S(1)} async-done(((bf16[4,6,128,256]{3,2,1,0:T(8,128)(2,1)}), bf16[4,6,128,256]{3,2,1,0:T(8,128)(2,1)S(1)}, u32[]{:S(2)}, u32[]{:S(2)}) %all-to-all-start.2) | async-done | bytes 1572896 | tf_op jit(solution)/shard_map/all_to_all | solution.py:315
  137.1 0.0 copy-start.1
  137.1 3.6 %all-to-all-start.3 = ((bf16[4,6,128,256]{3,2,1,0:T(8,128)(2,1)}), bf16[4,6,128,256]{3,2,1,0:T(8,128)(2,1)S(1)}, u32[]{:S(2)}, u32[]{:S(2)}) async-start(bf16[4,6,128,256]{3,2,1,0:T(8,128)(2,1)} %bitcast.29), calls=%async_computation.3 | async-start | bytes 3145728 | tf_op jit(solution)/shard_map/all_to_all | solution.py:315
  140.6 0.0 copy-start.6
  140.7 0.0 copy-start.7
  140.7 2.6 %add_multiply_fusion = f32[16,128,2]{2,1,0:T(8,128)} fusion(f32[16,128,2]{2,1,0:T(8,128)} %get-tuple-element.38, f32[16,128,2]{2,1,0:T(8,128)} %get-tuple-element.39), kind=kLoop, calls=%fused_computation | loop fusion | flops 8192 | bytes 49152 | tf_op jit(solution)/shard_map/div | solution.py:388
  143.3 0.0 copy-done.1
  143.3 2.2 %copy.17.gu_ref = f32[2,2048]{1,0:T(2,128)} copy(f32[2,2048]{0,1:T(8,128)} %bitcast.28) | data formatting | bytes 32768 | tf_op jit(solution)/shard_map/div | solution.py:388
  145.5 0.0 copy-done.6
  145.5 0.0 copy-done.7
  145.5 0.6 maximum_multiply_fusion.gt_ref
  146.1 25.0 %back.1.adj_ref.after_ref = f32[16,128,512]{2,1,0:T(8,128)} custom-call(s32[192]{0:T(256)} %get-tuple-element.28.look_ref, bf16[16,2,6,128,128]{4,3,2,1,0:T(8,128)(2,1)} %tiles_ref.7, bf16[16,2,128,512]{3,2,1,0:T(8,128)(2,1)} %get-tuple-element.35.scaled_ref), custom_call_target="tpu_custom_call" | custom-call | flops 3221225472 | bytes 14680064 | tf_op jit(solution)/shard_map/back/pallas_call | solution.py:374
  171.1 13.7 %sums.1 = (f32[2,2048]{1,0:T(2,128)}, f32[2,512]{1,0:T(2,128)}) custom-call(f32[2,2048]{1,0:T(2,128)} %copy.17.gu_ref, f32[2,512]{1,0:T(2,128)} %maximum_multiply_fusion.gt_ref, f32[16,128,512]{2,1,0:T(8,128)} %back.1.adj_ref.after_ref), custom_call_target="tpu_custom_call" | custom-call | bytes 8388608 | tf_op jit(solution)/shard_map/sums/pallas_call | solution.py:389
  184.8 3.9 %land.2.adj_ref = f32[16,128,512]{2,1,0:T(8,128)} custom-call(s32[4,1,128]{2,1,0:T(1,128)} %request.1.want_ref, f32[16,128,512]{2,1,0:T(8,128)} %back.1.adj_ref.after_ref, bf16[24,128,256]{2,1,0:T(8,128)(2,1)} %bitcast.26), custom_call_target="tpu_custom_call", output_to_operand_aliasing={{}: (1, {})} | custom-call | tf_op jit(solution)/shard_map/land/pallas_call | solution.py:406
  188.7 0.0 all-to-all-done.3
  188.7 0.0 copy-start.2
  188.7 1.2 copy-done.2
  189.8 0.0 copy-start.4
  189.8 0.0 copy-start.5
  189.8 3.9 %land.3 = f32[16,128,512]{2,1,0:T(8,128)} custom-call(s32[4,1,128]{2,1,0:T(1,128)} %request.1.want_ref, f32[16,128,512]{2,1,0:T(8,128)} %land.2.adj_ref, bf16[24,128,256]{2,1,0:T(8,128)(2,1)} %bitcast.27), custom_call_target="tpu_custom_call", output_to_operand_aliasing={{}: (1, {})} | custom-call | tf_op jit(solution)/shard_map/land/pallas_call | solution.py:406
  193.8 0.0 copy-done.4
  193.8 0.6 copy.24
  194.4 0.0 copy-done.5
  194.4 0.6 copy.25
Async XLA Ops:
  57.3 3.7 %copy-start.3 = (f32[2,2048]{1,0:T(2,128)S(1)}, f32[2,2048]{1,0:T(2,128)}, u32[]{:S(2)}) copy-start(f32[2,2048]{1,0:T(2,128)} %param.9) | copy-start | bytes 49156
  57.3 39.7 %all-to-all-start = ((bf16[4,6,128,256]{3,2,1,0:T(8,128)(2,1)}), bf16[4,6,128,256]{3,2,1,0:T(8,128)(2,1)S(1)}, u32[]{:S(2)}, u32[]{:S(2)}) async-start(bf16[4,6,128,256]{3,2,1,0:T(8,128)(2,1)} %bitcast.4), calls=%async_computation | async-start | bytes 3145728 | tf_op jit(solution)/shard_map/all_to_all | solution.py:315
  97.0 3.6 %copy-start = (bf16[4,6,128,256]{3,2,1,0:T(8,128)(2,1)}, bf16[4,6,128,256]{3,2,1,0:T(8,128)(2,1)S(1)}, u32[]{:S(2)}) copy-start(bf16[4,6,128,256]{3,2,1,0:T(8,128)(2,1)S(1)} %all-to-all-done) | copy-start | bytes 4718596
  97.0 40.1 %all-to-all-start.2 = ((bf16[4,6,128,256]{3,2,1,0:T(8,128)(2,1)}), bf16[4,6,128,256]{3,2,1,0:T(8,128)(2,1)S(1)}, u32[]{:S(2)}, u32[]{:S(2)}) async-start(bf16[4,6,128,256]{3,2,1,0:T(8,128)(2,1)} %bitcast.30), calls=%async_computation.2 | async-start | bytes 3145728 | tf_op jit(solution)/shard_map/all_to_all | solution.py:315
  137.1 6.2 %copy-start.1 = (bf16[4,6,128,256]{3,2,1,0:T(8,128)(2,1)}, bf16[4,6,128,256]{3,2,1,0:T(8,128)(2,1)S(1)}, u32[]{:S(2)}) copy-start(bf16[4,6,128,256]{3,2,1,0:T(8,128)(2,1)S(1)} %all-to-all-done.2) | copy-start | bytes 4718596
  137.1 51.6 %all-to-all-start.3 = ((bf16[4,6,128,256]{3,2,1,0:T(8,128)(2,1)}), bf16[4,6,128,256]{3,2,1,0:T(8,128)(2,1)S(1)}, u32[]{:S(2)}, u32[]{:S(2)}) async-start(bf16[4,6,128,256]{3,2,1,0:T(8,128)(2,1)} %bitcast.29), calls=%async_computation.3 | async-start | bytes 3145728 | tf_op jit(solution)/shard_map/all_to_all | solution.py:315
  140.6 4.8 %copy-start.6 = (f32[2,256]{1,0:T(2,128)S(1)}, f32[2,256]{1,0:T(2,128)}, u32[]{:S(2)}) copy-start(f32[2,256]{1,0:T(2,128)} %get-tuple-element.40) | copy-start | bytes 6148
  140.7 4.8 %copy-start.7 = (f32[2,256]{1,0:T(2,128)S(1)}, f32[2,256]{1,0:T(2,128)}, u32[]{:S(2)}) copy-start(f32[2,256]{1,0:T(2,128)} %get-tuple-element.41) | copy-start | bytes 6148
  188.7 1.2 copy-start.2
  189.8 3.9 %copy-start.4 = (f32[2,2048]{1,0:T(2,128)S(1)}, f32[2,2048]{1,0:T(2,128)}, u32[]{:S(2)}) copy-start(f32[2,2048]{1,0:T(2,128)} %get-tuple-element.50) | copy-start | bytes 49156
  189.8 4.5 %copy-start.5 = (f32[2,512]{1,0:T(2,128)S(1)}, f32[2,512]{1,0:T(2,128)}, u32[]{:S(2)}) copy-start(f32[2,512]{1,0:T(2,128)} %get-tuple-element.51) | copy-start | bytes 12292

commit v3 on v2

--- a/solution.py
+++ b/solution.py
@@ -20,7 +20,7 @@
     return pl.BlockSpec(shape, lambda *g: (0,) * len(shape))
 
 
-def plan_kernel(dims, me_ref, dest_ref, count_ref, req_ref, look_ref, start_ref, act_ref, pos_ref, slot_ref, fill):
+def plan_kernel(dims, me_ref, dest_ref, count_ref, req_ref, look_ref, from_ref, fill):
     B, A, M, D, cap = dims
     me = me_ref[0]
 
@@ -28,12 +28,12 @@
         fill[p] = 0
         for s in range(cap):
             req_ref[p, 0, s] = -1
+            from_ref[p * cap + s] = 0
         return carry
 
     lax.fori_loop(0, D, clear, 0)
 
-    def lists(i, total):
-        start_ref[i] = total
+    def lists(i, carry):
         for a in range(A):
             count = count_ref[a, i]
             for n in range(M):
@@ -43,21 +43,18 @@
                 block = dest - owner * B
                 used = n < count
                 look_ref[e] = jnp.where(used & (owner == me), block, -1)
-                far = used & (owner != me)
-
-                @pl.when(far)
+
+                @pl.when(used & (owner != me))
                 def _():
                     s = fill[owner]
+                    fill[owner] = s + 1
                     req_ref[owner, 0, s] = block
-                    fill[owner] = s + 1
-                    act_ref[total] = a
-                    pos_ref[total] = n
-                    slot_ref[total] = owner * cap + s
-
-                total = total + far.astype(jnp.int32)
-        return total
-
-    start_ref[B] = lax.fori_loop(0, B, lists, 0)
+                    from_ref[owner * cap + s] = e
+                    look_ref[e] = B + owner * cap + s
+
+        return carry
+
+    lax.fori_loop(0, B, lists, 0)
 
 
 def greet(axis, others):
@@ -114,52 +111,46 @@
         run(h, lambda c: c.wait())
 
 
-def near_kernel(G, A, M, look_ref, val_ref, tiles_ref, cont_ref):
-    for g in range(G):
-        i = pl.program_id(0) * G + g
-        for a in range(A):
-            weights, values = [], []
-            for n in range(M):
-                block = look_ref[(i * A + a) * M + n]
-                keep = jnp.where(block >= 0, 1.0, 0.0).astype(jnp.float32)
-                tile = tiles_ref[g, a, n]
-                weights.append(tile * jnp.full(tile.shape, keep, jnp.float32).astype(jnp.bfloat16))
-                values.append(val_ref[jnp.maximum(block, 0)])
-            cont_ref[g, a] = jnp.dot(
-                jnp.concatenate(weights, axis=1),
-                jnp.concatenate(values, axis=0),
-                preferred_element_type=jnp.float32,
-            )
-
-
 def transposed_dot(tile, right):
     return lax.dot_general(tile, right, (((0,), (0,)), ((), ())), preferred_element_type=jnp.float32)
 
 
+def continuation(M, first, look_ref, table, tiles):
+    weights, values = [], []
+    for n in range(M):
+        row = look_ref[first + n]
+        keep = jnp.where(row >= 0, 1.0, 0.0).astype(jnp.float32)
+        tile = tiles(n)
+        weights.append(tile * jnp.full(tile.shape, keep, jnp.float32).astype(jnp.bfloat16))
+        values.append(table[jnp.maximum(row, 0)])
+    return jnp.dot(
+        jnp.concatenate(weights, axis=1), jnp.concatenate(values, axis=0), preferred_element_type=jnp.float32
+    )
+
+
 def value_kernel(
-    G, rows, start_ref, act_ref, pos_ref, slot_ref, cont_ref, inc_ref, tiles_ref, cot_ref, util_ref, taste_ref, *rest
+    G, rows, col, look_ref, from_ref, val_ref, inc_ref, tiles_ref, cot_ref, util_ref, taste_ref, *rest
 ):
-    value_ref, scaled_ref, out_ref, gu_ref, gt_ref, acc = rest[-6:]
+    value_ref, scaled_ref, out_ref, gu_ref, gt_ref, acc, table, kept, sem = rest[-9:]
     step = pl.program_id(0)
+    _, A, M, R, _ = tiles_ref.shape
+    B, C, V = val_ref.shape[0], inc_ref.shape[0], inc_ref.shape[2]
 
     @pl.when(step == 0)
     def _():
         gt_ref[...] = jnp.zeros_like(gt_ref)
-
-    R = tiles_ref.shape[3]
-    acc[...] = cont_ref[...]
+        own = pltpu.make_async_copy(val_ref.at[:, :, pl.ds(col, V)], table.at[pl.ds(0, B)], sem.at[0])
+        far = pltpu.make_async_copy(inc_ref, table.at[pl.ds(B, C)], sem.at[1])
+        own.start()
+        far.start()
+        own.wait()
+        far.wait()
+
     t0, t1 = taste_ref[0:1, :], taste_ref[1:2, :]
     for g in range(G):
         i = step * G + g
-
-        def far(r, carry):
-            a = act_ref[r]
-            acc[g, a] += jnp.dot(
-                tiles_ref[g, a, pos_ref[r]], inc_ref[slot_ref[r]], preferred_element_type=jnp.float32
-            )
-            return carry
-
-        lax.fori_loop(start_ref[i], start_ref[i + 1], far, 0)
+        for a in range(A):
+            acc[g, a] = continuation(M, (i * A + a) * M, look_ref, table, lambda n: tiles_ref[i, a, n])
     for g in range(G):
         g0 = g1 = 0.0
         for c in range(0, R, rows):
@@ -184,15 +175,21 @@
             g0, g1 = g0 + h0, g1 + h1
         gt_ref[0:1, :] += jnp.sum(g0, axis=0, keepdims=True)
         gt_ref[1:2, :] += jnp.sum(g1, axis=0, keepdims=True)
-    for g in range(G):
-        i = step * G + g
-
-        def back(r, carry):
-            a = act_ref[r]
-            out_ref[slot_ref[r]] = transposed_dot(tiles_ref[g, a, pos_ref[r]], scaled_ref[g, a]).astype(jnp.bfloat16)
+    kept[pl.ds(step * G, G)] = scaled_ref[...]
+
+    @pl.when(step == pl.num_programs(0) - 1)
+    def _():
+        def back(q, carry):
+            for u in range(2):
+                slot = q * 2 + u
+                e = from_ref[slot]
+                pair = lax.div(e, M)
+                i = lax.div(pair, A)
+                a = pair - i * A
+                out_ref[slot] = transposed_dot(tiles_ref[i, a, e - pair * M], kept[i, a]).astype(jnp.bfloat16)
             return carry
 
-        lax.fori_loop(start_ref[i], start_ref[i + 1], back, 0)
+        lax.fori_loop(0, C // 2, back, 0)
 
 
 def back_kernel(G, A, M, look_ref, tiles_ref, scaled_ref, adj_ref):
@@ -208,12 +205,12 @@
             for n in range(M):
                 block = look_ref[(i * A + a) * M + n]
 
-                @pl.when(block >= 0)
+                @pl.when((block >= 0) & (block < adj_ref.shape[0]))
                 def _():
                     adj_ref[block] += transposed_dot(tiles_ref[g, a, n], scaled_ref[g, a])
 
 
-def sums_kernel(D, T, gu_ref, gt_ref, after_ref, ou_ref, ot_ref, lu, lt, us, ur, ts, tr):
+def sums_kernel(D, T, gu_ref, gt_ref, token_ref, after_ref, ou_ref, ot_ref, lu, lt, us, ur, ts, tr):
     ms, mt = lax.axis_index("state"), lax.axis_index("type")
     peers = [{"state": lax.rem(ms + k, D)} for k in range(1, D)]
     peers += [{"type": lax.rem(mt + k, T)} for k in range(1, T)]
@@ -250,7 +247,8 @@
 
 
 def land_kernel(D, cap, want_ref, adj_ref, ret_ref, *rest):
-    out_ref = rest[-1]
+    out_ref, done_ref = rest[-2:]
+    done_ref[0] = 0
     out_ref[...] = adj_ref[...]
 
     def peer(p, carry):
@@ -277,14 +275,11 @@
     shape = jax.ShapeDtypeStruct
     values = value_in.reshape(B, R, W)
 
-    req, look, start, act, pos, slot = pl.pallas_call(
+    req, look, origin = pl.pallas_call(
         functools.partial(plan_kernel, (B, A, M, D, cap)),
-        out_shape=(
-            shape((D, 1, 128), i32), shape((E,), i32), shape((B + 1,), i32),
-            shape((C,), i32), shape((C,), i32), shape((C,), i32),
-        ),
+        out_shape=(shape((D, 1, 128), i32), shape((E,), i32), shape((C,), i32)),
         in_specs=[smem()] * 3,
-        out_specs=[smem()] * 6,
+        out_specs=[smem()] * 3,
         scratch_shapes=[SMEM((D,), i32)],
         name="plan",
     )(lax.axis_index("state").reshape(1).astype(i32), dest_block.transpose(2, 1, 0), counts.T)
@@ -319,33 +314,21 @@
     incoming = [exchange(x) for x in outgoing]
 
     flops = 2 * E * R * R * W
-    cont = pl.pallas_call(
-        functools.partial(near_kernel, G, A, M),
-        grid=(B // G,),
-        out_shape=shape((B, A, R, W), f32),
-        in_specs=[smem(), whole((B, R, W)), pl.BlockSpec((G, A, M, R, R), lambda i: (i, 0, 0, 0, 0))],
-        out_specs=pl.BlockSpec((G, A, R, W), lambda i: (i, 0, 0, 0)),
-        cost_estimate=pl.CostEstimate(flops=flops, bytes_accessed=16 << 20, transcendentals=0),
-        name="near",
-    )(look, values, tiles)
-
     util_cols = state_util.reshape(A, B, R).transpose(1, 2, 0)
-    value = scaled = None
-    gus, gts, outbound = [], [], []
+    value = None
+    gus, gts, outbound, scaleds = [], [], [], []
     for h in range(H):
-        held = [] if h == 0 else [value, scaled]
+        held = [] if h == 0 else [value]
         value, scaled, out, gu, gt = pl.pallas_call(
-            functools.partial(value_kernel, G, 32),
+            functools.partial(value_kernel, G, 32, h * V),
             grid=(B // G,),
             out_shape=(
-                shape((B * R, W), f32), shape((B, A, R, W), bf16), shape((C, R, V), bf16),
+                shape((B * R, W), f32), shape((B, A, R, V), bf16), shape((C, R, V), bf16),
                 shape((B, R, A), f32), shape((A, V), f32),
             ),
-            in_specs=[smem()] * 4
-            + [
-                pl.BlockSpec((G, A, R, V), lambda i, h=h: (i, 0, 0, h)),
-                whole((C, R, V)),
-                pl.BlockSpec((G, A, M, R, R), lambda i: (i, 0, 0, 0, 0)),
+            in_specs=[
+                smem(), smem(), pl.BlockSpec(memory_space=pl.ANY), pl.BlockSpec(memory_space=pl.ANY),
+                whole((B, A, M, R, R)),
                 pl.BlockSpec((G * R, V), lambda i, h=h: (i, h)),
                 pl.BlockSpec((G, R, A), lambda i: (i, 0, 0)),
                 pl.BlockSpec((A, V), lambda i, h=h: (0, h)),
@@ -353,43 +336,68 @@
             + [pl.BlockSpec(memory_space=pl.ANY)] * len(held),
             out_specs=[
                 pl.BlockSpec((G * R, V), lambda i, h=h: (i, h)),
-                pl.BlockSpec((G, A, R, V), lambda i, h=h: (i, 0, 0, h)),
+                pl.BlockSpec((G, A, R, V), lambda i: (i, 0, 0, 0)),
                 whole((C, R, V)),
                 pl.BlockSpec((G, R, A), lambda i: (i, 0, 0)),
                 whole((A, V)),
             ],
-            input_output_aliases={10 + k: k for k in range(len(held))},
-            scratch_shapes=[VMEM((G, A, R, V), f32)],
+            input_output_aliases={8 + k: k for k in range(len(held))},
+            scratch_shapes=[
+                VMEM((G, A, R, V), f32), VMEM((B + C, R, V), bf16), VMEM((B, A, R, V), bf16),
+                pltpu.SemaphoreType.DMA((2,)),
+            ],
             cost_estimate=pl.CostEstimate(
-                flops=flops // (4 * H), bytes_accessed=(30 << 20) // H, transcendentals=3 * B * R * V
+                flops=flops // H, bytes_accessed=(24 << 20) // H, transcendentals=3 * B * R * V
             ),
             name="value",
-        )(start, act, pos, slot, cont, incoming[h], tiles, cotangent, util_cols, taste, *held)
+        )(look, origin, values, incoming[h], tiles, cotangent, util_cols, taste, *held)
         outbound.append(out)
+        scaleds.append(scaled)
         gus.append(gu)
         gts.append(gt)
 
-    returned = [exchange(x) for x in outbound]
-
-    adj = pl.pallas_call(
-        functools.partial(back_kernel, G, A, M),
-        grid=(B // G,),
-        out_shape=shape((B, R, W), f32),
-        in_specs=[
-            smem(),
-            pl.BlockSpec((G, A, M, R, R), lambda i: (i, 0, 0, 0, 0)),
-            pl.BlockSpec((G, A, R, W), lambda i: (i, 0, 0, 0)),
-        ],
-        out_specs=whole((B, R, W)),
-        cost_estimate=pl.CostEstimate(flops=flops, bytes_accessed=14 << 20, transcendentals=0),
-        name="back",
-    )(look, tiles, scaled)
-
+    adjs = [
+        pl.pallas_call(
+            functools.partial(back_kernel, G, A, M),
+            grid=(B // G,),
+            out_shape=shape((B, R, V), f32),
+            in_specs=[
+                smem(),
+                pl.BlockSpec((G, A, M, R, R), lambda i: (i, 0, 0, 0, 0)),
+                pl.BlockSpec((G, A, R, V), lambda i: (i, 0, 0, 0)),
+            ],
+            out_specs=whole((B, R, V)),
+            cost_estimate=pl.CostEstimate(flops=flops // H, bytes_accessed=(14 << 20) // H, transcendentals=0),
+            name="back",
+        )(look, tiles, x)
+        for x in scaleds
+    ]
+
+    returned = []
+    for h in range(H):
+        if h > 0:
+            outbound[h], adjs[h - 1] = lax.optimization_barrier((outbound[h], adjs[h - 1]))
+        returned.append(exchange(outbound[h]))
+
+    adjoint, tokens = None, []
     gu_rows = sum(gus).transpose(2, 0, 1).reshape(A, B * R) / (W * T)
+    for h in range(H):
+        held = [] if h == 0 else [adjoint]
+        adjoint, token = pl.pallas_call(
+            functools.partial(land_kernel, D, cap),
+            grid=(1,),
+            out_shape=(shape((B, R, W), f32), shape((1,), i32)),
+            in_specs=[smem(), whole((B, R, V)), whole((C, R, V))]
+            + [pl.BlockSpec(memory_space=pl.ANY)] * len(held),
+            out_specs=[pl.BlockSpec((B, R, V), lambda j, h=h: (0, 0, h)), smem()],
+            input_output_aliases={3 + k: k for k in range(len(held))},
+            name="land",
+        )(wanted, adjs[h], returned[h], *held)
+        tokens.append(token)
     grad_util, grad_taste = pl.pallas_call(
         functools.partial(sums_kernel, D, T),
         out_shape=(shape((A, B * R), f32), shape((A, W), f32)),
-        in_specs=[pl.BlockSpec(memory_space=VMEM)] * 2 + [pl.BlockSpec(memory_space=pl.ANY)],
+        in_specs=[pl.BlockSpec(memory_space=VMEM)] * 2 + [smem(), pl.BlockSpec(memory_space=pl.ANY)],
         out_specs=[pl.BlockSpec(memory_space=VMEM)] * 2,
         scratch_shapes=[
             VMEM((T, A, B * R), f32), VMEM((D, A, W), f32),
@@ -399,19 +407,8 @@
         compiler_params=pltpu.CompilerParams(collective_id=1, has_side_effects=True),
         cost_estimate=pl.CostEstimate(flops=0, bytes_accessed=8 << 20, transcendentals=0),
         name="sums",
-    )(gu_rows, jnp.concatenate(gts, axis=1) / (B * R * D), adj)
-
-    adjoint = adj
-    for h in range(H):
-        adjoint = pl.pallas_call(
-            functools.partial(land_kernel, D, cap),
-            grid=(1,),
-            out_shape=shape((B, R, W), f32),
-            in_specs=[smem(), pl.BlockSpec((B, R, V), lambda j, h=h: (0, 0, h)), whole((C, R, V))],
-            out_specs=pl.BlockSpec((B, R, V), lambda j, h=h: (0, 0, h)),
-            input_output_aliases={1: 0},
-            name="land",
-        )(wanted, adjoint, returned[h])
+    )(gu_rows, jnp.concatenate(gts, axis=1) / (B * R * D), tokens[0], adjs[-1])
+
     return value, adjoint.reshape(B * R, W), grad_util, grad_taste
 
 

time: 194 us -> 198 us (1.021); the launches traced: 195 us -> 196 us
  waiting for transfers between devices: 26.8 us -> 21.4 us
  starting transfers between devices: 10.8 us -> 15.5 us
    pallas_call x1 -> x2, Pallas kernels: 25 us -> 41.3 us  [local(): pl.pallas_call(functools.partial(back_kernel, G, A, M), grid=(B // G,), o...]
    pallas_call x3 -> x2, Pallas kernels: 44.3 us -> 29.1 us  [local(): pl.pallas_call(functools.partial(value_kernel, G, 32, h * V), grid=(B //...]
    all_to_all x3, waiting for transfers between devices: 26.8 us -> 21.4 us  [exchange(): lax.all_to_all(x.reshape(D, cap, R, V), 'state', split_axis=0, concat_axi...]
    all_to_all x3, starting transfers between devices: 10.8 us -> 15.5 us  [exchange(): lax.all_to_all(x.reshape(D, cap, R, V), 'state', split_axis=0, concat_axi...]
where the time goes in v3:
time: 198 us; the launch traced here: 196 us
  Pallas kernels  108 us (55%)
  blocking collectives  40.5 us (20%)
  waiting for transfers between devices  21.4 us (11%)
  starting transfers between devices  15.5 us (8%)
  local copies, waits for them, and re-layouts  5.89 us (3%)
  other arithmetic  3.33 us (2%)
    pallas_call x2, Pallas kernels, local(): pl.pallas_call(functools.partial(back_kernel, G, A, M), grid=(B // G,), o...  41.3 us
    all_to_all x1, blocking collectives, exchange(): lax.all_to_all(x.reshape(D, cap, R, V), 'state', split_axis=0, concat_axi...  40.5 us
    pallas_call x2, Pallas kernels, local(): pl.pallas_call(functools.partial(value_kernel, G, 32, h * V), grid=(B //...  29.1 us
    all_to_all x3, waiting for transfers between devices, exchange(): lax.all_to_all(x.reshape(D, cap, R, V), 'state', split_axis=0, concat_axi...  21.4 us
    all_to_all x3, starting transfers between devices, exchange(): lax.all_to_all(x.reshape(D, cap, R, V), 'state', split_axis=0, concat_axi...  15.5 us
    pallas_call x1, Pallas kernels, local(): pl.pallas_call(functools.partial(sums_kernel, D, T), out_shape=(shape((A,...  14 us
    pallas_call x1, Pallas kernels, local(): pl.pallas_call(functools.partial(request_kernel, D), out_shape=shape((D,...  8.55 us
    pallas_call x2, Pallas kernels, local(): pl.pallas_call(functools.partial(land_kernel, D, cap), grid=(1,), out_sha...  7.79 us
  transfers between devices with their start and end apart: 3, of which 2 were waited for; matrix products, arithmetic and copies ran while one was open for 3% of the time, Pallas kernels for 45%

profile of v3, /device:TPU:0, one launch (start us, length us, event | category | flops | bytes accessed | tf_op | source)
XLA Modules:
  0.0 195.6 jit_solution(14480372776436595158)
XLA Ops:
  0.6 3.8 %plan.1 = (s32[4,1,128]{2,1,0:T(1,128)}, s32[192]{0:T(256)}, s32[24]{0:T(128)}) custom-call(s32[1]{0:T(128)} %bitcast.me_ref, s32[6,2,16]{2,1,0:T(2,128)} %bitcast.33, s32[2,16]{1,0:T(2,128)} %bitcast.34), custom_call_target="tpu_custom_call" | custom-call | tf_op jit(solution)/shard_map/plan/pallas_call | solution.py:278
  4.5 8.6 %request.1.want_ref = s32[4,1,128]{2,1,0:T(1,128)} custom-call(s32[4,1,128]{2,1,0:T(1,128)} %get-tuple-element.28.req_ref), custom_call_target="tpu_custom_call" | custom-call | tf_op jit(solution)/shard_map/request/pallas_call | solution.py:287
  13.0 3.7 %gather.1 = (bf16[24,128,256]{2,1,0:T(8,128)(2,1)}, bf16[24,128,256]{2,1,0:T(8,128)(2,1)}) custom-call(s32[4,1,128]{2,1,0:T(1,128)} %request.1.want_ref, bf16[16,128,512]{2,1,0:T(8,128)(2,1)} %bitcast.19), custom_call_target="tpu_custom_call" | custom-call | tf_op jit(solution)/shard_map/gather/pallas_call | solution.py:300
  16.7 40.5 %all_to_all.20 = bf16[4,6,128,256]{3,2,1,0:T(8,128)(2,1)} all-to-all(bf16[4,6,128,256]{3,2,1,0:T(8,128)(2,1)} %bitcast.32), channel_id=1, replica_groups=mesh['groups'=2,'state'=4,'type'=4] {'state'}, dimensions={0} | all-to-all | bytes 3145728 | tf_op jit(solution)/shard_map/all_to_all | solution.py:310
  57.2 0.0 copy-start.3
  57.2 3.7 %all-to-all-start = ((bf16[4,6,128,256]{3,2,1,0:T(8,128)(2,1)}), bf16[4,6,128,256]{3,2,1,0:T(8,128)(2,1)S(1)}, u32[]{:S(2)}, u32[]{:S(2)}) async-start(bf16[4,6,128,256]{3,2,1,0:T(8,128)(2,1)} %bitcast.4), calls=%async_computation | async-start | bytes 3145728 | tf_op jit(solution)/shard_map/all_to_all | solution.py:310
  60.9 0.0 copy-done.3
  60.9 1.3 copy.13
  62.2 14.5 %value.2 = (f32[2048,512]{1,0:T(8,128)}, bf16[16,2,128,256]{3,2,1,0:T(8,128)(2,1)}, bf16[24,128,256]{2,1,0:T(8,128)(2,1)}, f32[16,128,2]{2,1,0:T(8,128)}, f32[2,256]{1,0:T(2,128)}) custom-call(s32[192]{0:T(256)} %get-tuple-element.26.look_ref, s32[24]{0:T(128)} %get-tuple-element.27.from_ref, bf16[16,128,512]{2,1,0:T(8,128)(2,1)} %bitcast.20, ...), custom_call_target="tpu_custom_call" | custom-call | flops 1610612736 | bytes 12582912 | tf_op jit(solution)/shard_map/value/pallas_call | solution.py:322
  76.8 20.1 %all-to-all-done = bf16[4,6,128,256]{3,2,1,0:T(8,128)(2,1)S(1)} async-done(((bf16[4,6,128,256]{3,2,1,0:T(8,128)(2,1)}), bf16[4,6,128,256]{3,2,1,0:T(8,128)(2,1)S(1)}, u32[]{:S(2)}, u32[]{:S(2)}) %all-to-all-start) | async-done | bytes 1572896 | tf_op jit(solution)/shard_map/all_to_all | solution.py:310
  96.9 0.0 copy-start.1
  96.9 3.6 %all-to-all-start.3 = ((bf16[4,6,128,256]{3,2,1,0:T(8,128)(2,1)}), bf16[4,6,128,256]{3,2,1,0:T(8,128)(2,1)S(1)}, u32[]{:S(2)}, u32[]{:S(2)}) async-start(bf16[4,6,128,256]{3,2,1,0:T(8,128)(2,1)} %bitcast.31), calls=%async_computation.3 | async-start | bytes 3145728 | tf_op jit(solution)/shard_map/all_to_all | solution.py:310
  100.5 20.6 %back.3.adj_ref = f32[16,128,256]{2,1,0:T(8,128)} custom-call(s32[192]{0:T(256)} %get-tuple-element.26.look_ref, bf16[16,2,6,128,128]{4,3,2,1,0:T(8,128)(2,1)} %tiles_ref.7, bf16[16,2,128,256]{3,2,1,0:T(8,128)(2,1)} %get-tuple-element.35.scaled_ref), custom_call_target="tpu_custom_call" | custom-call | flops 1610612736 | bytes 7340032 | tf_op jit(solution)/shard_map/back/pallas_call | solution.py:360
  121.1 0.0 copy-done.1
  121.1 14.6 %value.3 = (f32[2048,512]{1,0:T(8,128)}, bf16[16,2,128,256]{3,2,1,0:T(8,128)(2,1)}, bf16[24,128,256]{2,1,0:T(8,128)(2,1)}, f32[16,128,2]{2,1,0:T(8,128)}, f32[2,256]{1,0:T(2,128)}) custom-call(s32[192]{0:T(256)} %get-tuple-element.26.look_ref, s32[24]{0:T(128)} %get-tuple-element.27.from_ref, ...), custom_call_target="tpu_custom_call", output_to_operand_aliasing={{0}: (8, {})} | custom-call | flops 1610612736 | bytes 12582912 | tf_op jit(solution)/shard_map/value/pallas_call | solution.py:322
  135.7 1.3 all-to-all-done.3
  137.0 0.0 copy-start
  137.0 8.3 %all-to-all-start.2 = ((bf16[4,6,128,256]{3,2,1,0:T(8,128)(2,1)}), bf16[4,6,128,256]{3,2,1,0:T(8,128)(2,1)S(1)}, u32[]{:S(2)}, u32[]{:S(2)}) async-start(bf16[4,6,128,256]{3,2,1,0:T(8,128)(2,1)} %bitcast.30), calls=%async_computation.2 | async-start | bytes 3145728 | tf_op jit(solution)/shard_map/all_to_all | solution.py:310
  145.3 0.0 copy-start.6
  145.3 0.0 copy-start.7
  145.3 2.7 %add_multiply_fusion = f32[16,128,2]{2,1,0:T(8,128)} fusion(f32[16,128,2]{2,1,0:T(8,128)} %get-tuple-element.41, f32[16,128,2]{2,1,0:T(8,128)} %get-tuple-element.42), kind=kLoop, calls=%fused_computation | loop fusion | flops 8192 | bytes 49152 | tf_op jit(solution)/shard_map/div | solution.py:383
  148.0 0.0 copy-done
  148.0 2.2 %copy.15.gu_ref = f32[2,2048]{1,0:T(2,128)} copy(f32[2,2048]{0,1:T(8,128)} %bitcast.28) | data formatting | bytes 32768 | tf_op jit(solution)/shard_map/div | solution.py:383
  150.2 0.0 copy-done.6
  150.2 0.0 copy-done.7
  150.2 0.6 maximum_multiply_fusion.gt_ref
  150.8 20.6 %back.2.adj_ref.after_ref = f32[16,128,256]{2,1,0:T(8,128)} custom-call(s32[192]{0:T(256)} %get-tuple-element.26.look_ref, bf16[16,2,6,128,128]{4,3,2,1,0:T(8,128)(2,1)} %tiles_ref.7, bf16[16,2,128,256]{3,2,1,0:T(8,128)(2,1)} %get-tuple-element.33.scaled_ref), custom_call_target="tpu_custom_call" | custom-call | flops 1610612736 | bytes 7340032 | tf_op jit(solution)/shard_map/back/pallas_call | solution.py:360
  171.4 3.9 %land.2 = (f32[16,128,512]{2,1,0:T(8,128)}, s32[1]{0:T(128)}) custom-call(s32[4,1,128]{2,1,0:T(1,128)} %request.1.want_ref, f32[16,128,256]{2,1,0:T(8,128)} %back.3.adj_ref, bf16[24,128,256]{2,1,0:T(8,128)(2,1)} %bitcast.24), custom_call_target="tpu_custom_call" | custom-call | tf_op jit(solution)/shard_map/land/pallas_call | solution.py:386
  175.3 14.0 %sums.1 = (f32[2,2048]{1,0:T(2,128)}, f32[2,512]{1,0:T(2,128)}) custom-call(f32[2,2048]{1,0:T(2,128)} %copy.15.gu_ref, f32[2,512]{1,0:T(2,128)} %maximum_multiply_fusion.gt_ref, s32[1]{0:T(128)} %get-tuple-element.45.token_ref, f32[16,128,256]{2,1,0:T(8,128)} %back.2.adj_ref.after_ref), custom_call_target="tpu_custom_call" | custom-call | bytes 8388608 | tf_op jit(solution)/shard_map/sums/pallas_call | solution.py:397
  189.3 0.0 all-to-all-done.2
  189.3 0.0 copy-start.2
  189.3 1.2 copy-done.2
  190.5 0.0 copy-start.4
  190.5 0.0 copy-start.5
  190.5 3.9 %land.3 = (f32[16,128,512]{2,1,0:T(8,128)}, s32[1]{0:T(128)}) custom-call(s32[4,1,128]{2,1,0:T(1,128)} %request.1.want_ref, f32[16,128,256]{2,1,0:T(8,128)} %back.2.adj_ref.after_ref, bf16[24,128,256]{2,1,0:T(8,128)(2,1)} %bitcast.27, f32[16,128,512]{2,1,0:T(8,128)} %get-tuple-element.39.rest_0_), custom_call_target="tpu_custom_call", output_to_operand_aliasing={{0}: (3, {})} | custom-call | tf_op jit(solution)/shard_map/land/pallas_call | solution.py:386
  194.4 0.0 copy-done.4
  194.4 0.6 copy.20
  195.0 0.0 copy-done.5
  195.0 0.6 copy.21
Async XLA Ops:
  57.2 3.7 %copy-start.3 = (f32[2,2048]{1,0:T(2,128)S(1)}, f32[2,2048]{1,0:T(2,128)}, u32[]{:S(2)}) copy-start(f32[2,2048]{1,0:T(2,128)} %param.9) | copy-start | bytes 49156
  57.2 39.7 %all-to-all-start = ((bf16[4,6,128,256]{3,2,1,0:T(8,128)(2,1)}), bf16[4,6,128,256]{3,2,1,0:T(8,128)(2,1)S(1)}, u32[]{:S(2)}, u32[]{:S(2)}) async-start(bf16[4,6,128,256]{3,2,1,0:T(8,128)(2,1)} %bitcast.4), calls=%async_computation | async-start | bytes 3145728 | tf_op jit(solution)/shard_map/all_to_all | solution.py:310
  96.9 24.2 %copy-start.1 = (bf16[4,6,128,256]{3,2,1,0:T(8,128)(2,1)}, bf16[4,6,128,256]{3,2,1,0:T(8,128)(2,1)S(1)}, u32[]{:S(2)}) copy-start(bf16[4,6,128,256]{3,2,1,0:T(8,128)(2,1)S(1)} %all-to-all-done) | copy-start | bytes 4718596
  96.9 40.1 %all-to-all-start.3 = ((bf16[4,6,128,256]{3,2,1,0:T(8,128)(2,1)}), bf16[4,6,128,256]{3,2,1,0:T(8,128)(2,1)S(1)}, u32[]{:S(2)}, u32[]{:S(2)}) async-start(bf16[4,6,128,256]{3,2,1,0:T(8,128)(2,1)} %bitcast.31), calls=%async_computation.3 | async-start | bytes 3145728 | tf_op jit(solution)/shard_map/all_to_all | solution.py:310
  137.0 11.0 %copy-start = (bf16[4,6,128,256]{3,2,1,0:T(8,128)(2,1)}, bf16[4,6,128,256]{3,2,1,0:T(8,128)(2,1)S(1)}, u32[]{:S(2)}) copy-start(bf16[4,6,128,256]{3,2,1,0:T(8,128)(2,1)S(1)} %all-to-all-done.3) | copy-start | bytes 4718596
  137.0 52.3 %all-to-all-start.2 = ((bf16[4,6,128,256]{3,2,1,0:T(8,128)(2,1)}), bf16[4,6,128,256]{3,2,1,0:T(8,128)(2,1)S(1)}, u32[]{:S(2)}, u32[]{:S(2)}) async-start(bf16[4,6,128,256]{3,2,1,0:T(8,128)(2,1)} %bitcast.30), calls=%async_computation.2 | async-start | bytes 3145728 | tf_op jit(solution)/shard_map/all_to_all | solution.py:310
  145.3 4.9 %copy-start.6 = (f32[2,256]{1,0:T(2,128)S(1)}, f32[2,256]{1,0:T(2,128)}, u32[]{:S(2)}) copy-start(f32[2,256]{1,0:T(2,128)} %get-tuple-element.43) | copy-start | bytes 6148
  145.3 4.9 %copy-start.7 = (f32[2,256]{1,0:T(2,128)S(1)}, f32[2,256]{1,0:T(2,128)}, u32[]{:S(2)}) copy-start(f32[2,256]{1,0:T(2,128)} %get-tuple-element.44) | copy-start | bytes 6148
  189.3 1.2 copy-start.2
  190.5 3.9 %copy-start.4 = (f32[2,2048]{1,0:T(2,128)S(1)}, f32[2,2048]{1,0:T(2,128)}, u32[]{:S(2)}) copy-start(f32[2,2048]{1,0:T(2,128)} %get-tuple-element.54) | copy-start | bytes 49156
  190.5 4.5 %copy-start.5 = (f32[2,512]{1,0:T(2,128)S(1)}, f32[2,512]{1,0:T(2,128)}, u32[]{:S(2)}) copy-start(f32[2,512]{1,0:T(2,128)} %get-tuple-element.55) | copy-start | bytes 12292

commit v4 on v3

--- a/solution.py
+++ b/solution.py
@@ -128,23 +128,89 @@
     )
 
 
+def fetch_value_kernel(G, rows, D, look_ref, from_ref, val_ref, *rest):
+    H = (len(rest) - 14) // 2
+    outs, rest = rest[:H], rest[H:]
+    body, lands = rest[:9], rest[9 : 9 + H - 1]
+    acc, table, kept, sem, send, recv = rest[9 + H - 1 :]
+    step = pl.program_id(0)
+    B, C, V = val_ref.shape[0], outs[0].shape[0], outs[0].shape[2]
+    cap = C // D
+    me = lax.axis_index("state")
+
+    def copy(h, k):
+        to = lax.rem(me + k, D)
+        land = table.at[pl.ds(B + me * cap, cap)] if h == 0 else lands[h - 1].at[pl.ds(me * cap, cap)]
+        return pltpu.make_async_remote_copy(
+            src_ref=outs[h].at[pl.ds(to * cap, cap)],
+            dst_ref=land,
+            send_sem=send.at[h, k],
+            recv_sem=recv.at[h, k],
+            device_id={"state": to},
+            device_id_type=MESH,
+        )
+
+    @pl.when(step == 0)
+    def _():
+        greet("state", [{"state": lax.rem(me + k, D)} for k in range(1, D)])
+        for h in range(H):
+            for k in range(1, D):
+                copy(h, k).start()
+        own = pltpu.make_async_copy(val_ref.at[:, :, pl.ds(0, V)], table.at[pl.ds(0, B)], sem.at[0])
+        mine = pltpu.make_async_copy(
+            outs[0].at[pl.ds(me * cap, cap)], table.at[pl.ds(B + me * cap, cap)], sem.at[1]
+        )
+        own.start()
+        mine.start()
+        own.wait()
+        mine.wait()
+        for k in range(1, D):
+            copy(0, k).wait()
+
+    work(G, rows, look_ref, from_ref, *body, acc, table, kept)
+
+    @pl.when(step == pl.num_programs(0) - 1)
+    def _():
+        for h in range(1, H):
+            for k in range(1, D):
+                copy(h, k).wait()
+
+
 def value_kernel(
     G, rows, col, look_ref, from_ref, val_ref, inc_ref, tiles_ref, cot_ref, util_ref, taste_ref, *rest
 ):
+    before_ref = rest[0]
     value_ref, scaled_ref, out_ref, gu_ref, gt_ref, acc, table, kept, sem = rest[-9:]
     step = pl.program_id(0)
-    _, A, M, R, _ = tiles_ref.shape
     B, C, V = val_ref.shape[0], inc_ref.shape[0], inc_ref.shape[2]
 
     @pl.when(step == 0)
     def _():
-        gt_ref[...] = jnp.zeros_like(gt_ref)
         own = pltpu.make_async_copy(val_ref.at[:, :, pl.ds(col, V)], table.at[pl.ds(0, B)], sem.at[0])
         far = pltpu.make_async_copy(inc_ref, table.at[pl.ds(B, C)], sem.at[1])
         own.start()
         far.start()
         own.wait()
         far.wait()
+
+    value_ref[:, :col] = before_ref[...]
+    work(
+        G, rows, look_ref, from_ref, tiles_ref, cot_ref, util_ref, taste_ref,
+        value_ref.at[:, col:], scaled_ref, out_ref, gu_ref, gt_ref, acc, table, kept,
+    )
+
+
+def work(
+    G, rows, look_ref, from_ref, tiles_ref, cot_ref, util_ref, taste_ref,
+    value_ref, scaled_ref, out_ref, gu_ref, gt_ref, acc, table, kept,
+):
+    step = pl.program_id(0)
+    _, A, M, R, _ = tiles_ref.shape
+    C = out_ref.shape[0]
+
+    @pl.when(step == 0)
+    def _():
+        gt_ref[...] = jnp.zeros_like(gt_ref)
 
     t0, t1 = taste_ref[0:1, :], taste_ref[1:2, :]
     for g in range(G):
@@ -193,6 +259,7 @@
 
 
 def back_kernel(G, A, M, look_ref, tiles_ref, scaled_ref, adj_ref):
+    spare = adj_ref.shape[0] - 1
     step = pl.program_id(0)
 
     @pl.when(step == 0)
@@ -204,10 +271,8 @@
         for a in range(A):
             for n in range(M):
                 block = look_ref[(i * A + a) * M + n]
-
-                @pl.when((block >= 0) & (block < adj_ref.shape[0]))
-                def _():
-                    adj_ref[block] += transposed_dot(tiles_ref[g, a, n], scaled_ref[g, a])
+                here = jnp.where((block >= 0) & (block < spare), block, spare)
+                adj_ref[here] += transposed_dot(tiles_ref[g, a, n], scaled_ref[g, a])
 
 
 def sums_kernel(D, T, gu_ref, gt_ref, token_ref, after_ref, ou_ref, ot_ref, lu, lt, us, ur, ts, tr):
@@ -311,46 +376,61 @@
             x.reshape(D, cap, R, V), "state", split_axis=0, concat_axis=0, tiled=True
         ).reshape(C, R, V)
 
-    incoming = [exchange(x) for x in outgoing]
+    incoming = []
 
     flops = 2 * E * R * R * W
     util_cols = state_util.reshape(A, B, R).transpose(1, 2, 0)
     value = None
     gus, gts, outbound, scaleds = [], [], [], []
+    any_spec = pl.BlockSpec(memory_space=pl.ANY)
     for h in range(H):
-        held = [] if h == 0 else [value]
-        value, scaled, out, gu, gt = pl.pallas_call(
-            functools.partial(value_kernel, G, 32, h * V),
-            grid=(B // G,),
-            out_shape=(
-                shape((B * R, W), f32), shape((B, A, R, V), bf16), shape((C, R, V), bf16),
-                shape((B, R, A), f32), shape((A, V), f32),
-            ),
-            in_specs=[
-                smem(), smem(), pl.BlockSpec(memory_space=pl.ANY), pl.BlockSpec(memory_space=pl.ANY),
-                whole((B, A, M, R, R)),
-                pl.BlockSpec((G * R, V), lambda i, h=h: (i, h)),
-                pl.BlockSpec((G, R, A), lambda i: (i, 0, 0)),
-                pl.BlockSpec((A, V), lambda i, h=h: (0, h)),
-            ]
-            + [pl.BlockSpec(memory_space=pl.ANY)] * len(held),
-            out_specs=[
-                pl.BlockSpec((G * R, V), lambda i, h=h: (i, h)),
-                pl.BlockSpec((G, A, R, V), lambda i: (i, 0, 0, 0)),
-                whole((C, R, V)),
-                pl.BlockSpec((G, R, A), lambda i: (i, 0, 0)),
-                whole((A, V)),
-            ],
-            input_output_aliases={8 + k: k for k in range(len(held))},
-            scratch_shapes=[
-                VMEM((G, A, R, V), f32), VMEM((B + C, R, V), bf16), VMEM((B, A, R, V), bf16),
-                pltpu.SemaphoreType.DMA((2,)),
-            ],
-            cost_estimate=pl.CostEstimate(
-                flops=flops // H, bytes_accessed=(24 << 20) // H, transcendentals=3 * B * R * V
-            ),
-            name="value",
-        )(look, origin, values, incoming[h], tiles, cotangent, util_cols, taste, *held)
+        wide = V * (h + 1)
+        ins = [
+            whole((B, A, M, R, R)),
+            pl.BlockSpec((G * R, V), lambda i, h=h: (i, h)),
+            pl.BlockSpec((G, R, A), lambda i: (i, 0, 0)),
+            pl.BlockSpec((A, V), lambda i, h=h: (0, h)),
+        ]
+        out_shape = [
+            shape((B * R, wide), f32), shape((B, A, R, V), bf16), shape((C, R, V), bf16),
+            shape((B, R, A), f32), shape((A, V), f32),
+        ]
+        out_specs = [
+            pl.BlockSpec((G * R, wide), lambda i: (i, 0)),
+            pl.BlockSpec((G, A, R, V), lambda i: (i, 0, 0, 0)),
+            whole((C, R, V)),
+            pl.BlockSpec((G, R, A), lambda i: (i, 0, 0)),
+            whole((A, V)),
+        ]
+        scratch = [
+            VMEM((G, A, R, V), f32), VMEM((B + C, R, V), bf16), VMEM((B, A, R, V), bf16),
+            pltpu.SemaphoreType.DMA((2,)),
+        ]
+        cost = pl.CostEstimate(flops=flops // H, bytes_accessed=(24 << 20) // H, transcendentals=3 * B * R * V)
+        if h == 0:
+            value, scaled, out, gu, gt, *incoming = pl.pallas_call(
+                functools.partial(fetch_value_kernel, G, 32, D),
+                grid=(B // G,),
+                out_shape=out_shape + [shape((C, R, V), bf16)] * (H - 1),
+                in_specs=[smem(), smem(), any_spec] + [any_spec] * H + ins,
+                out_specs=out_specs + [any_spec] * (H - 1),
+                scratch_shapes=scratch + [pltpu.SemaphoreType.DMA((H, D)), pltpu.SemaphoreType.DMA((H, D))],
+                compiler_params=pltpu.CompilerParams(collective_id=2, has_side_effects=True),
+                cost_estimate=cost,
+                name="fetch",
+            )(look, origin, values, *outgoing, tiles, cotangent, util_cols, taste)
+        else:
+            value, scaled, out, gu, gt = pl.pallas_call(
+                functools.partial(value_kernel, G, 32, h * V),
+                grid=(B // G,),
+                out_shape=out_shape,
+                in_specs=[smem(), smem(), any_spec, any_spec] + ins
+                + [pl.BlockSpec((G * R, h * V), lambda i: (i, 0))],
+                out_specs=out_specs,
+                scratch_shapes=scratch,
+                cost_estimate=cost,
+                name="value",
+            )(look, origin, values, incoming[h - 1], tiles, cotangent, util_cols, taste, value)
         outbound.append(out)
         scaleds.append(scaled)
         gus.append(gu)
@@ -360,13 +440,13 @@
         pl.pallas_call(
             functools.partial(back_kernel, G, A, M),
             grid=(B // G,),
-            out_shape=shape((B, R, V), f32),
+            out_shape=shape((B + 1, R, V), f32),
             in_specs=[
                 smem(),
                 pl.BlockSpec((G, A, M, R, R), lambda i: (i, 0, 0, 0, 0)),
                 pl.BlockSpec((G, A, R, V), lambda i: (i, 0, 0, 0)),
             ],
-            out_specs=whole((B, R, V)),
+            out_specs=whole((B + 1, R, V)),
             cost_estimate=pl.CostEstimate(flops=flops // H, bytes_accessed=(14 << 20) // H, transcendentals=0),
             name="back",
         )(look, tiles, x)

time: 198 us -> 182 us (0.919)
  blocking collectives: 40.5 us -> 0 us
  Pallas kernels: 108 us -> 143 us
  waiting for transfers between devices: 21.4 us -> 12.1 us
    pallas_call x0 -> x1, Pallas kernels: none -> 67.4 us  [local(): pl.pallas_call(functools.partial(fetch_value_kernel, G, 32, D), grid=(B /...]
    all_to_all x1 -> x0, blocking collectives: 40.5 us -> none  [exchange(): lax.all_to_all(x.reshape(D, cap, R, V), 'state', split_axis=0, concat_axi...]
    pallas_call x2, Pallas kernels: 41.3 us -> 15.6 us  [local(): pl.pallas_call(functools.partial(back_kernel, G, A, M), grid=(B // G,), o...]
    pallas_call x2 -> x1, Pallas kernels: 29.1 us -> 15.6 us  [local(): pl.pallas_call(functools.partial(value_kernel, G, 32, h * V), grid=(B //...]
    all_to_all x3 -> x2, waiting for transfers between devices: 21.4 us -> 12.1 us  [exchange(): lax.all_to_all(x.reshape(D, cap, R, V), 'state', split_axis=0, concat_axi...]
    pallas_call x1, Pallas kernels: 14 us -> 20.4 us  [local(): pl.pallas_call(functools.partial(sums_kernel, D, T), out_shape=(shape((A,...]
    unnamed x19 -> x15, local copies, waits for them, and re-layouts: 3.73 us -> 4.47 us
    all_to_all x3 -> x2, starting transfers between devices: 15.5 us -> 15.4 us  [exchange(): lax.all_to_all(x.reshape(D, cap, R, V), 'state', split_axis=0, concat_axi...]
  transfers between devices with their start and end apart: 3 -> 2, of which waited for: 2 -> 1; matrix products, arithmetic and copies ran while one was open for 3% -> 3% of each run, Pallas kernels for 45% -> 31%
where the time goes in v4:
time: 182 us; the launch traced here: 181 us
  Pallas kernels  143 us (79%)
  starting transfers between devices  15.4 us (8%)
  waiting for transfers between devices  12.1 us (7%)
  local copies, waits for them, and re-layouts  6.62 us (4%)
  other arithmetic  3.26 us (2%)
    pallas_call x1, Pallas kernels, local(): pl.pallas_call(functools.partial(fetch_value_kernel, G, 32, D), grid=(B /...  67.4 us
    pallas_call x1, Pallas kernels, local(): pl.pallas_call(functools.partial(sums_kernel, D, T), out_shape=(shape((A,...  20.4 us
    pallas_call x2, Pallas kernels, local(): pl.pallas_call(functools.partial(back_kernel, G, A, M), grid=(B // G,), o...  15.6 us
    pallas_call x1, Pallas kernels, local(): pl.pallas_call(functools.partial(value_kernel, G, 32, h * V), grid=(B //...  15.6 us
    all_to_all x2, starting transfers between devices, exchange(): lax.all_to_all(x.reshape(D, cap, R, V), 'state', split_axis=0, concat_axi...  15.4 us
    all_to_all x2, waiting for transfers between devices, exchange(): lax.all_to_all(x.reshape(D, cap, R, V), 'state', split_axis=0, concat_axi...  12.1 us
    pallas_call x1, Pallas kernels, local(): pl.pallas_call(functools.partial(request_kernel, D), out_shape=shape((D,...  8.54 us
    pallas_call x2, Pallas kernels, local(): pl.pallas_call(functools.partial(land_kernel, D, cap), grid=(1,), out_sha...  7.81 us
  transfers between devices with their start and end apart: 2, of which 1 were waited for; matrix products, arithmetic and copies ran while one was open for 3% of the time, Pallas kernels for 31%

profile of v4, /device:TPU:0, one launch (start us, length us, event | category | flops | bytes accessed | tf_op | source)
XLA Modules:
  0.0 180.9 jit_solution(16488702021539600345)
XLA Ops:
  0.6 3.8 %plan.1 = (s32[4,1,128]{2,1,0:T(1,128)}, s32[192]{0:T(256)}, s32[24]{0:T(128)}) custom-call(s32[1]{0:T(128)} %bitcast.me_ref, s32[6,2,16]{2,1,0:T(2,128)} %bitcast.26, s32[2,16]{1,0:T(2,128)} %bitcast.27), custom_call_target="tpu_custom_call" | custom-call | tf_op jit(solution)/shard_map/plan/pallas_call | solution.py:343
  4.5 8.5 %request.1.want_ref = s32[4,1,128]{2,1,0:T(1,128)} custom-call(s32[4,1,128]{2,1,0:T(1,128)} %get-tuple-element.29.req_ref), custom_call_target="tpu_custom_call" | custom-call | tf_op jit(solution)/shard_map/request/pallas_call | solution.py:352
  13.0 2.1 %copy.12 = f32[2,2048]{0,1:T(8,128)} copy(f32[2,2048]{1,0:T(2,128)} %param.9) | data formatting | bytes 32768 | tf_op args[2]
  15.1 3.7 %gather.1 = (bf16[24,128,256]{2,1,0:T(8,128)(2,1)}, bf16[24,128,256]{2,1,0:T(8,128)(2,1)}) custom-call(s32[4,1,128]{2,1,0:T(1,128)} %request.1.want_ref, bf16[16,128,512]{2,1,0:T(8,128)(2,1)} %bitcast.15), custom_call_target="tpu_custom_call" | custom-call | tf_op jit(solution)/shard_map/gather/pallas_call | solution.py:365
  18.7 67.4 %fetch.1 = (f32[2048,256]{1,0:T(8,128)}, bf16[16,2,128,256]{3,2,1,0:T(8,128)(2,1)}, bf16[24,128,256]{2,1,0:T(8,128)(2,1)}, f32[16,128,2]{2,1,0:T(8,128)}, f32[2,...) custom-call(s32[192]{0:T(256)} %get-tuple-element.27.look_ref, s32[24]{0:T(128)} %get-tuple-element.28.from_ref, ...), custom_call_target="tpu_custom_call" | custom-call | flops 1610612736 | bytes 12582912 | tf_op jit(solution)/shard_map/fetch/pallas_call | solution.py:411
  86.1 11.9 %all-to-all-start.1 = ((bf16[4,6,128,256]{3,2,1,0:T(8,128)(2,1)}), bf16[4,6,128,256]{3,2,1,0:T(8,128)(2,1)S(1)}, u32[]{:S(2)}, u32[]{:S(2)}) async-start(bf16[4,6,128,256]{3,2,1,0:T(8,128)(2,1)} %bitcast.25), calls=%async_computation.1 | async-start | bytes 3145728 | tf_op jit(solution)/shard_map/all_to_all | solution.py:375
  98.0 7.8 %back.3.adj_ref = f32[17,128,256]{2,1,0:T(8,128)} custom-call(s32[192]{0:T(256)} %get-tuple-element.27.look_ref, bf16[16,2,6,128,128]{4,3,2,1,0:T(8,128)(2,1)} %tiles_ref.5, bf16[16,2,128,256]{3,2,1,0:T(8,128)(2,1)} %get-tuple-element.37.scaled_ref), custom_call_target="tpu_custom_call" | custom-call | flops 1610612736 | bytes 7340032 | tf_op jit(solution)/shard_map/back/pallas_call | solution.py:440
  105.8 15.6 %value.1 = (f32[2048,512]{1,0:T(8,128)}, bf16[16,2,128,256]{3,2,1,0:T(8,128)(2,1)}, bf16[24,128,256]{2,1,0:T(8,128)(2,1)}, f32[16,128,2]{2,1,0:T(8,128)}, f32[2,256]{1,0:T(2,128)}) custom-call(s32[192]{0:T(256)} %get-tuple-element.27.look_ref, s32[24]{0:T(128)} %get-tuple-element.28.from_ref, bf16[16,128,512]{2,1,0:T(8,128)(2,1)} %bitcast.17, ...), custom_call_target="tpu_custom_call" | custom-call | flops 1610612736 | bytes 12582912 | tf_op jit(solution)/shard_map/value/pallas_call | solution.py:423
  121.4 12.1 %all-to-all-done.1 = bf16[4,6,128,256]{3,2,1,0:T(8,128)(2,1)S(1)} async-done(((bf16[4,6,128,256]{3,2,1,0:T(8,128)(2,1)}), bf16[4,6,128,256]{3,2,1,0:T(8,128)(2,1)S(1)}, u32[]{:S(2)}, u32[]{:S(2)}) %all-to-all-start.1) | async-done | bytes 1572896 | tf_op jit(solution)/shard_map/all_to_all | solution.py:375
  133.5 0.0 copy-start
  133.5 3.6 %all-to-all-start = ((bf16[4,6,128,256]{3,2,1,0:T(8,128)(2,1)}), bf16[4,6,128,256]{3,2,1,0:T(8,128)(2,1)S(1)}, u32[]{:S(2)}, u32[]{:S(2)}) async-start(bf16[4,6,128,256]{3,2,1,0:T(8,128)(2,1)} %bitcast.24), calls=%async_computation | async-start | bytes 3145728 | tf_op jit(solution)/shard_map/all_to_all | solution.py:375
  137.0 0.0 copy-start.4
  137.0 0.0 copy-start.5
  137.1 2.7 %add_multiply_fusion = f32[16,128,2]{2,1,0:T(8,128)} fusion(f32[16,128,2]{2,1,0:T(8,128)} %get-tuple-element.43, f32[16,128,2]{2,1,0:T(8,128)} %get-tuple-element.44), kind=kLoop, calls=%fused_computation | loop fusion | flops 8192 | bytes 49152 | tf_op jit(solution)/shard_map/div | solution.py:463
  139.7 0.0 copy-done
  139.7 2.2 %copy.14.gu_ref = f32[2,2048]{1,0:T(2,128)} copy(f32[2,2048]{0,1:T(8,128)} %bitcast.22) | data formatting | bytes 32768 | tf_op jit(solution)/shard_map/div | solution.py:463
  141.9 0.0 copy-done.4
  141.9 0.0 copy-done.5
  141.9 0.6 maximum_multiply_fusion.gt_ref
  142.5 7.8 %back.2.adj_ref.after_ref = f32[17,128,256]{2,1,0:T(8,128)} custom-call(s32[192]{0:T(256)} %get-tuple-element.27.look_ref, bf16[16,2,6,128,128]{4,3,2,1,0:T(8,128)(2,1)} %tiles_ref.5, bf16[16,2,128,256]{3,2,1,0:T(8,128)(2,1)} %get-tuple-element.35.scaled_ref), custom_call_target="tpu_custom_call" | custom-call | flops 1610612736 | bytes 7340032 | tf_op jit(solution)/shard_map/back/pallas_call | solution.py:440
  150.3 3.9 %land.2 = (f32[16,128,512]{2,1,0:T(8,128)}, s32[1]{0:T(128)}) custom-call(s32[4,1,128]{2,1,0:T(1,128)} %request.1.want_ref, f32[17,128,256]{2,1,0:T(8,128)} %back.3.adj_ref, bf16[24,128,256]{2,1,0:T(8,128)(2,1)} %bitcast.20), custom_call_target="tpu_custom_call" | custom-call | tf_op jit(solution)/shard_map/land/pallas_call | solution.py:466
  154.2 20.4 %sums.1 = (f32[2,2048]{1,0:T(2,128)}, f32[2,512]{1,0:T(2,128)}) custom-call(f32[2,2048]{1,0:T(2,128)} %copy.14.gu_ref, f32[2,512]{1,0:T(2,128)} %maximum_multiply_fusion.gt_ref, s32[1]{0:T(128)} %get-tuple-element.47.token_ref, f32[17,128,256]{2,1,0:T(8,128)} %back.2.adj_ref.after_ref), custom_call_target="tpu_custom_call" | custom-call | bytes 8388608 | tf_op jit(solution)/shard_map/sums/pallas_call | solution.py:477
  174.6 0.0 all-to-all-done
  174.6 0.0 copy-start.1
  174.6 1.2 copy-done.1
  175.8 0.0 copy-start.2
  175.8 0.0 copy-start.3
  175.8 3.9 %land.3 = (f32[16,128,512]{2,1,0:T(8,128)}, s32[1]{0:T(128)}) custom-call(s32[4,1,128]{2,1,0:T(1,128)} %request.1.want_ref, f32[17,128,256]{2,1,0:T(8,128)} %back.2.adj_ref.after_ref, bf16[24,128,256]{2,1,0:T(8,128)(2,1)} %bitcast.21, f32[16,128,512]{2,1,0:T(8,128)} %get-tuple-element.41.rest_0_), custom_call_target="tpu_custom_call", output_to_operand_aliasing={{0}: (3, {})} | custom-call | tf_op jit(solution)/shard_map/land/pallas_call | solution.py:466
  179.7 0.0 copy-done.2
  179.7 0.6 copy.18
  180.3 0.0 copy-done.3
  180.3 0.6 copy.19
Async XLA Ops:
  86.1 47.3 %all-to-all-start.1 = ((bf16[4,6,128,256]{3,2,1,0:T(8,128)(2,1)}), bf16[4,6,128,256]{3,2,1,0:T(8,128)(2,1)S(1)}, u32[]{:S(2)}, u32[]{:S(2)}) async-start(bf16[4,6,128,256]{3,2,1,0:T(8,128)(2,1)} %bitcast.25), calls=%async_computation.1 | async-start | bytes 3145728 | tf_op jit(solution)/shard_map/all_to_all | solution.py:375
  133.5 6.3 %copy-start = (bf16[4,6,128,256]{3,2,1,0:T(8,128)(2,1)}, bf16[4,6,128,256]{3,2,1,0:T(8,128)(2,1)S(1)}, u32[]{:S(2)}) copy-start(bf16[4,6,128,256]{3,2,1,0:T(8,128)(2,1)S(1)} %all-to-all-done.1) | copy-start | bytes 4718596
  133.5 41.1 %all-to-all-start = ((bf16[4,6,128,256]{3,2,1,0:T(8,128)(2,1)}), bf16[4,6,128,256]{3,2,1,0:T(8,128)(2,1)S(1)}, u32[]{:S(2)}, u32[]{:S(2)}) async-start(bf16[4,6,128,256]{3,2,1,0:T(8,128)(2,1)} %bitcast.24), calls=%async_computation | async-start | bytes 3145728 | tf_op jit(solution)/shard_map/all_to_all | solution.py:375
  137.0 4.8 %copy-start.4 = (f32[2,256]{1,0:T(2,128)S(1)}, f32[2,256]{1,0:T(2,128)}, u32[]{:S(2)}) copy-start(f32[2,256]{1,0:T(2,128)} %get-tuple-element.45) | copy-start | bytes 6148
  137.0 4.8 %copy-start.5 = (f32[2,256]{1,0:T(2,128)S(1)}, f32[2,256]{1,0:T(2,128)}, u32[]{:S(2)}) copy-start(f32[2,256]{1,0:T(2,128)} %get-tuple-element.46) | copy-start | bytes 6148
  174.6 1.2 copy-start.1
  175.8 3.9 %copy-start.2 = (f32[2,2048]{1,0:T(2,128)S(1)}, f32[2,2048]{1,0:T(2,128)}, u32[]{:S(2)}) copy-start(f32[2,2048]{1,0:T(2,128)} %get-tuple-element.56) | copy-start | bytes 49156
  175.8 4.5 %copy-start.3 = (f32[2,512]{1,0:T(2,128)S(1)}, f32[2,512]{1,0:T(2,128)}, u32[]{:S(2)}) copy-start(f32[2,512]{1,0:T(2,128)} %get-tuple-element.57) | copy-start | bytes 12292

commit v5 on v4

--- a/solution.py
+++ b/solution.py
@@ -219,12 +219,14 @@
             acc[g, a] = continuation(M, (i * A + a) * M, look_ref, table, lambda n: tiles_ref[i, a, n])
     for g in range(G):
         g0 = g1 = 0.0
+        cols = [
+            jnp.transpose(jnp.broadcast_to(util_ref[a : a + 1, g * R : (g + 1) * R], (R, R))) for a in range(A)
+        ]
         for c in range(0, R, rows):
             at = slice(c, c + rows)
             here = slice(g * R + c, g * R + c + rows)
-            util = util_ref[g, at, :]
-            q0 = util[:, 0:1] + t0 + 0.95 * acc[g, 0, at, :]
-            q1 = util[:, 1:2] + t1 + 0.95 * acc[g, 1, at, :]
+            q0 = cols[0][at, 0:1] + t0 + 0.95 * acc[g, 0, at, :]
+            q1 = cols[1][at, 0:1] + t1 + 0.95 * acc[g, 1, at, :]
             gap = q1 - q0
             small = jnp.exp(-jnp.abs(gap))
             total = 1.0 + small
@@ -379,7 +381,6 @@
     incoming = []
 
     flops = 2 * E * R * R * W
-    util_cols = state_util.reshape(A, B, R).transpose(1, 2, 0)
     value = None
     gus, gts, outbound, scaleds = [], [], [], []
     any_spec = pl.BlockSpec(memory_space=pl.ANY)
@@ -388,7 +389,7 @@
         ins = [
             whole((B, A, M, R, R)),
             pl.BlockSpec((G * R, V), lambda i, h=h: (i, h)),
-            pl.BlockSpec((G, R, A), lambda i: (i, 0, 0)),
+            pl.BlockSpec((A, G * R), lambda i: (0, i)),
             pl.BlockSpec((A, V), lambda i, h=h: (0, h)),
         ]
         out_shape = [
@@ -418,7 +419,7 @@
                 compiler_params=pltpu.CompilerParams(collective_id=2, has_side_effects=True),
                 cost_estimate=cost,
                 name="fetch",
-            )(look, origin, values, *outgoing, tiles, cotangent, util_cols, taste)
+            )(look, origin, values, *outgoing, tiles, cotangent, state_util, taste)
         else:
             value, scaled, out, gu, gt = pl.pallas_call(
                 functools.partial(value_kernel, G, 32, h * V),
@@ -430,7 +431,7 @@
                 scratch_shapes=scratch,
                 cost_estimate=cost,
                 name="value",
-            )(look, origin, values, incoming[h - 1], tiles, cotangent, util_cols, taste, value)
+            )(look, origin, values, incoming[h - 1], tiles, cotangent, state_util, taste, value)
         outbound.append(out)
         scaleds.append(scaled)
         gus.append(gu)

time: 182 us -> 179 us (0.984)
  waiting for transfers between devices: 12.1 us -> 9.51 us
  local copies, waits for them, and re-layouts: 6.62 us -> 4.55 us
  Pallas kernels: 143 us -> 145 us
    all_to_all x2, waiting for transfers between devices: 12.1 us -> 9.51 us  [exchange(): lax.all_to_all(x.reshape(D, cap, R, V), 'state', split_axis=0, concat_axi...]
    pallas_call x1, Pallas kernels: 15.6 us -> 18.1 us  [local(): pl.pallas_call(functools.partial(value_kernel, G, 32, h * V), grid=(B //...]
    unnamed x15 -> x14, local copies, waits for them, and re-layouts: 4.47 us -> 2.39 us
  transfers between devices with their start and end apart: 2 -> 2, of which waited for: 1 -> 1; matrix products, arithmetic and copies ran while one was open for 3% -> 3% of each run, Pallas kernels for 31% -> 32%
where the time goes in v5:
time: 179 us
  Pallas kernels  145 us (81%)
  starting transfers between devices  15.4 us (9%)
  waiting for transfers between devices  9.51 us (5%)
  local copies, waits for them, and re-layouts  4.55 us (3%)
  other arithmetic  3.34 us (2%)
    pallas_call x1, Pallas kernels, local(): pl.pallas_call(functools.partial(fetch_value_kernel, G, 32, D), grid=(B /...  67.3 us
    pallas_call x1, Pallas kernels, local(): pl.pallas_call(functools.partial(sums_kernel, D, T), out_shape=(shape((A,...  20.3 us
    pallas_call x1, Pallas kernels, local(): pl.pallas_call(functools.partial(value_kernel, G, 32, h * V), grid=(B //...  18.1 us
    pallas_call x2, Pallas kernels, local(): pl.pallas_call(functools.partial(back_kernel, G, A, M), grid=(B // G,), o...  15.6 us
    all_to_all x2, starting transfers between devices, exchange(): lax.all_to_all(x.reshape(D, cap, R, V), 'state', split_axis=0, concat_axi...  15.4 us
    all_to_all x2, waiting for transfers between devices, exchange(): lax.all_to_all(x.reshape(D, cap, R, V), 'state', split_axis=0, concat_axi...  9.51 us
    pallas_call x1, Pallas kernels, local(): pl.pallas_call(functools.partial(request_kernel, D), out_shape=shape((D,...  8.55 us
    pallas_call x2, Pallas kernels, local(): pl.pallas_call(functools.partial(land_kernel, D, cap), grid=(1,), out_sha...  7.81 us
  transfers between devices with their start and end apart: 2, of which 1 were waited for; matrix products, arithmetic and copies ran while one was open for 3% of the time, Pallas kernels for 32%

profile of v5, /device:TPU:0, one launch (start us, length us, event | category | flops | bytes accessed | tf_op | source)
XLA Modules:
  0.0 178.8 jit_solution(5393748414620599471)
XLA Ops:
  0.6 3.8 %plan.1 = (s32[4,1,128]{2,1,0:T(1,128)}, s32[192]{0:T(256)}, s32[24]{0:T(128)}) custom-call(s32[1]{0:T(128)} %bitcast.me_ref, s32[6,2,16]{2,1,0:T(2,128)} %bitcast.21, s32[2,16]{1,0:T(2,128)} %bitcast.22), custom_call_target="tpu_custom_call" | custom-call | tf_op jit(solution)/shard_map/plan/pallas_call | solution.py:345
  4.5 8.6 %request.1.want_ref = s32[4,1,128]{2,1,0:T(1,128)} custom-call(s32[4,1,128]{2,1,0:T(1,128)} %get-tuple-element.29.req_ref), custom_call_target="tpu_custom_call" | custom-call | tf_op jit(solution)/shard_map/request/pallas_call | solution.py:354
  13.0 3.7 %gather.1 = (bf16[24,128,256]{2,1,0:T(8,128)(2,1)}, bf16[24,128,256]{2,1,0:T(8,128)(2,1)}) custom-call(s32[4,1,128]{2,1,0:T(1,128)} %request.1.want_ref, bf16[16,128,512]{2,1,0:T(8,128)(2,1)} %bitcast.12), custom_call_target="tpu_custom_call" | custom-call | tf_op jit(solution)/shard_map/gather/pallas_call | solution.py:367
  16.7 67.3 %fetch.1 = (f32[2048,256]{1,0:T(8,128)}, bf16[16,2,128,256]{3,2,1,0:T(8,128)(2,1)}, bf16[24,128,256]{2,1,0:T(8,128)(2,1)}, f32[16,128,2]{2,1,0:T(8,128)}, f32[2,...) custom-call(s32[192]{0:T(256)} %get-tuple-element.27.look_ref, s32[24]{0:T(128)} %get-tuple-element.28.from_ref, ...), custom_call_target="tpu_custom_call" | custom-call | flops 1610612736 | bytes 12582912 | tf_op jit(solution)/shard_map/fetch/pallas_call | solution.py:412
  84.0 11.9 %all-to-all-start.1 = ((bf16[4,6,128,256]{3,2,1,0:T(8,128)(2,1)}), bf16[4,6,128,256]{3,2,1,0:T(8,128)(2,1)S(1)}, u32[]{:S(2)}, u32[]{:S(2)}) async-start(bf16[4,6,128,256]{3,2,1,0:T(8,128)(2,1)} %bitcast.20), calls=%async_computation.1 | async-start | bytes 3145728 | tf_op jit(solution)/shard_map/all_to_all | solution.py:377
  95.9 7.8 %back.3.adj_ref = f32[17,128,256]{2,1,0:T(8,128)} custom-call(s32[192]{0:T(256)} %get-tuple-element.27.look_ref, bf16[16,2,6,128,128]{4,3,2,1,0:T(8,128)(2,1)} %tiles_ref.5, bf16[16,2,128,256]{3,2,1,0:T(8,128)(2,1)} %get-tuple-element.37.scaled_ref), custom_call_target="tpu_custom_call" | custom-call | flops 1610612736 | bytes 7340032 | tf_op jit(solution)/shard_map/back/pallas_call | solution.py:441
  103.7 18.1 %value.1 = (f32[2048,512]{1,0:T(8,128)}, bf16[16,2,128,256]{3,2,1,0:T(8,128)(2,1)}, bf16[24,128,256]{2,1,0:T(8,128)(2,1)}, f32[16,128,2]{2,1,0:T(8,128)}, f32[2,256]{1,0:T(2,128)}) custom-call(s32[192]{0:T(256)} %get-tuple-element.27.look_ref, s32[24]{0:T(128)} %get-tuple-element.28.from_ref, bf16[16,128,512]{2,1,0:T(8,128)(2,1)} %bitcast.14, ...), custom_call_target="tpu_custom_call" | custom-call | flops 1610612736 | bytes 12582912 | tf_op jit(solution)/shard_map/value/pallas_call | solution.py:424
  121.8 9.5 %all-to-all-done.1 = bf16[4,6,128,256]{3,2,1,0:T(8,128)(2,1)S(1)} async-done(((bf16[4,6,128,256]{3,2,1,0:T(8,128)(2,1)}), bf16[4,6,128,256]{3,2,1,0:T(8,128)(2,1)S(1)}, u32[]{:S(2)}, u32[]{:S(2)}) %all-to-all-start.1) | async-done | bytes 1572896 | tf_op jit(solution)/shard_map/all_to_all | solution.py:377
  131.3 0.0 copy-start
  131.3 3.6 %all-to-all-start = ((bf16[4,6,128,256]{3,2,1,0:T(8,128)(2,1)}), bf16[4,6,128,256]{3,2,1,0:T(8,128)(2,1)S(1)}, u32[]{:S(2)}, u32[]{:S(2)}) async-start(bf16[4,6,128,256]{3,2,1,0:T(8,128)(2,1)} %bitcast.19), calls=%async_computation | async-start | bytes 3145728 | tf_op jit(solution)/shard_map/all_to_all | solution.py:377
  134.9 0.0 copy-start.4
  134.9 0.0 copy-start.5
  134.9 2.7 %add_multiply_fusion = f32[16,128,2]{2,1,0:T(8,128)} fusion(f32[16,128,2]{2,1,0:T(8,128)} %get-tuple-element.43, f32[16,128,2]{2,1,0:T(8,128)} %get-tuple-element.44), kind=kLoop, calls=%fused_computation | loop fusion | flops 8192 | bytes 49152 | tf_op jit(solution)/shard_map/div | solution.py:464
  137.7 0.0 copy-done
  137.7 2.2 %copy.13.gu_ref = f32[2,2048]{1,0:T(2,128)} copy(f32[2,2048]{0,1:T(8,128)} %bitcast.17) | data formatting | bytes 32768 | tf_op jit(solution)/shard_map/div | solution.py:464
  139.8 0.0 copy-done.4
  139.8 0.0 copy-done.5
  139.8 0.6 maximum_multiply_fusion.gt_ref
  140.4 7.8 %back.2.adj_ref.after_ref = f32[17,128,256]{2,1,0:T(8,128)} custom-call(s32[192]{0:T(256)} %get-tuple-element.27.look_ref, bf16[16,2,6,128,128]{4,3,2,1,0:T(8,128)(2,1)} %tiles_ref.5, bf16[16,2,128,256]{3,2,1,0:T(8,128)(2,1)} %get-tuple-element.35.scaled_ref), custom_call_target="tpu_custom_call" | custom-call | flops 1610612736 | bytes 7340032 | tf_op jit(solution)/shard_map/back/pallas_call | solution.py:441
  148.2 3.9 %land.2 = (f32[16,128,512]{2,1,0:T(8,128)}, s32[1]{0:T(128)}) custom-call(s32[4,1,128]{2,1,0:T(1,128)} %request.1.want_ref, f32[17,128,256]{2,1,0:T(8,128)} %back.3.adj_ref, bf16[24,128,256]{2,1,0:T(8,128)(2,1)} %bitcast.15), custom_call_target="tpu_custom_call" | custom-call | tf_op jit(solution)/shard_map/land/pallas_call | solution.py:467
  152.1 20.3 %sums.1 = (f32[2,2048]{1,0:T(2,128)}, f32[2,512]{1,0:T(2,128)}) custom-call(f32[2,2048]{1,0:T(2,128)} %copy.13.gu_ref, f32[2,512]{1,0:T(2,128)} %maximum_multiply_fusion.gt_ref, s32[1]{0:T(128)} %get-tuple-element.47.token_ref, f32[17,128,256]{2,1,0:T(8,128)} %back.2.adj_ref.after_ref), custom_call_target="tpu_custom_call" | custom-call | bytes 8388608 | tf_op jit(solution)/shard_map/sums/pallas_call | solution.py:478
  172.5 0.0 all-to-all-done
  172.5 0.0 copy-start.1
  172.5 1.2 copy-done.1
  173.7 0.0 copy-start.2
  173.7 0.0 copy-start.3
  173.7 3.9 %land.3 = (f32[16,128,512]{2,1,0:T(8,128)}, s32[1]{0:T(128)}) custom-call(s32[4,1,128]{2,1,0:T(1,128)} %request.1.want_ref, f32[17,128,256]{2,1,0:T(8,128)} %back.2.adj_ref.after_ref, bf16[24,128,256]{2,1,0:T(8,128)(2,1)} %bitcast.16, f32[16,128,512]{2,1,0:T(8,128)} %get-tuple-element.41.rest_0_), custom_call_target="tpu_custom_call", output_to_operand_aliasing={{0}: (3, {})} | custom-call | tf_op jit(solution)/shard_map/land/pallas_call | solution.py:467
  177.6 0.0 copy-done.2
  177.6 0.6 copy.17
  178.2 0.0 copy-done.3
  178.2 0.6 copy.18
Async XLA Ops:
  84.0 47.3 %all-to-all-start.1 = ((bf16[4,6,128,256]{3,2,1,0:T(8,128)(2,1)}), bf16[4,6,128,256]{3,2,1,0:T(8,128)(2,1)S(1)}, u32[]{:S(2)}, u32[]{:S(2)}) async-start(bf16[4,6,128,256]{3,2,1,0:T(8,128)(2,1)} %bitcast.20), calls=%async_computation.1 | async-start | bytes 3145728 | tf_op jit(solution)/shard_map/all_to_all | solution.py:377
  131.3 6.3 %copy-start = (bf16[4,6,128,256]{3,2,1,0:T(8,128)(2,1)}, bf16[4,6,128,256]{3,2,1,0:T(8,128)(2,1)S(1)}, u32[]{:S(2)}) copy-start(bf16[4,6,128,256]{3,2,1,0:T(8,128)(2,1)S(1)} %all-to-all-done.1) | copy-start | bytes 4718596
  131.3 41.1 %all-to-all-start = ((bf16[4,6,128,256]{3,2,1,0:T(8,128)(2,1)}), bf16[4,6,128,256]{3,2,1,0:T(8,128)(2,1)S(1)}, u32[]{:S(2)}, u32[]{:S(2)}) async-start(bf16[4,6,128,256]{3,2,1,0:T(8,128)(2,1)} %bitcast.19), calls=%async_computation | async-start | bytes 3145728 | tf_op jit(solution)/shard_map/all_to_all | solution.py:377
  134.9 4.9 %copy-start.4 = (f32[2,256]{1,0:T(2,128)S(1)}, f32[2,256]{1,0:T(2,128)}, u32[]{:S(2)}) copy-start(f32[2,256]{1,0:T(2,128)} %get-tuple-element.45) | copy-start | bytes 6148
  134.9 4.9 %copy-start.5 = (f32[2,256]{1,0:T(2,128)S(1)}, f32[2,256]{1,0:T(2,128)}, u32[]{:S(2)}) copy-start(f32[2,256]{1,0:T(2,128)} %get-tuple-element.46) | copy-start | bytes 6148
  172.5 1.2 copy-start.1
  173.7 3.9 %copy-start.2 = (f32[2,2048]{1,0:T(2,128)S(1)}, f32[2,2048]{1,0:T(2,128)}, u32[]{:S(2)}) copy-start(f32[2,2048]{1,0:T(2,128)} %get-tuple-element.56) | copy-start | bytes 49156
  173.7 4.5 %copy-start.3 = (f32[2,512]{1,0:T(2,128)S(1)}, f32[2,512]{1,0:T(2,128)}, u32[]{:S(2)}) copy-start(f32[2,512]{1,0:T(2,128)} %get-tuple-element.57) | copy-start | bytes 12292
